TPU v7x, 256 devices: a whole 4x4x8 slice. The times are simulated.
256 devices in a mesh: blk: 16 (over x, y_lo, core), grp: 16 (over z, y_hi).
Axes of the slice: x: 4, y: 4 (y_hi: 2, y_lo: 2; y = y_hi * 2 + y_lo), z: 8, core: 2. Of those that a mesh axis runs over, the one named last changes fastest.
Arguments:
- phase_space: float32 [6, 32768], P(None, 'blk'), may hold values from -3.5 to 3.5
- force_rates: float32 [6, 32768], P(None, 'blk'), may hold values from -4 to 4
- irregular: float32 [6, 32768], P(None, 'blk'), may hold values from -3 to 3
- stellar_masses: float32 [32768], P('blk'), may hold values from 9.155274e-06 to 9.1552734e-05
- levels: int32 [256], P('blk'), may hold values from 0 to 3, as said below
- active: int32 [4, 256], P(None, 'blk'), may hold values from 0 to 1, as said below
- partner: int32 [256], P('blk'), may hold values from 0 to 255, as said below
Outputs:
- kinematics: float32 [6, 32768], P(None, 'blk')
- combined_force: float32 [6, 32768], P(None, 'blk')
- irregular_force: float32 [6, 32768], P(None, 'blk')
Inputs may be any that keep to these rules, and one draw needn't show every extreme that they name: levels of 0 to 3; in every shard 2 to 4 blocks have level 0, at most 6 level 1 or less and at most 8 level 2 or less, and some shard has exactly 4, 6 and 8. active[n, b] is 1 exactly when n + 1 is a multiple of 2 ** levels[b]. partner is mutual (the partner of partner[b] is b) and has the same place within its shard; the blocks of one shard have exactly 1 partner on each shard, their own shard included, where the one block is its own partner.
All inputs are finite; a program needn't handle non-finite values.
Results may differ from a plain program's by a relative error of at most 0.0003.
Values sent between devices are 32-bit elements; how exact they have to be, the bound alone decides.
No kernel may reach another device: no remote copies, remote signals or barrier semaphores. Data moves between devices by JAX's collectives and lax.ppermute only.
A program may use at most 64 MiB of HBM per device.

v0:
```python
import functools
import jax
import jax.numpy as jnp
from jax import lax
from jax.experimental import pallas as pl
from jax.experimental.pallas import tpu as pltpu
from jax.sharding import PartitionSpec as P

WIDE = 0.04
CLOSE = 0.0001
TICK = 0.125
NB = 16
BS = 128
W = NB * BS
F32 = jnp.float32
CAPS = (4, 6, 4, 8)
TOP = (0, 1, 0, 2)
SENT = (-1, 0, 1, 1)
SLOTS = (0, 4, 8, 8)

VMEM = pl.BlockSpec(memory_space=pltpu.VMEM)
SMEM = pl.BlockSpec(memory_space=pltpu.SMEM)


def pair(target, source, mass, soften, acc):
    r = [source[c] - target[c] for c in range(3)]
    w = [source[c] - target[c] for c in range(3, 6)]
    d = (r[0] * r[0] + soften) + r[1] * r[1] + r[2] * r[2]
    s = lax.rsqrt(d)
    s2 = s * s
    weight = (mass * s) * s2
    q = (r[0] * w[0] + r[1] * w[1] + r[2] * w[2]) * (s2 * 3.0)
    acc = list(acc)
    for c in range(3):
        acc[c] = acc[c] + weight * r[c]
        acc[3 + c] = acc[3 + c] + weight * (w[c] - q * r[c])
    return tuple(acc)


def pair_split(target, source, mass, acc):
    r = [source[c] - target[c] for c in range(3)]
    w = [source[c] - target[c] for c in range(3, 6)]
    dd = r[0] * r[0] + r[1] * r[1] + r[2] * r[2]
    rw = (r[0] * w[0] + r[1] * w[1] + r[2] * w[2]) * 3.0
    acc = list(acc)
    for soften, sign in ((CLOSE, 1.0), (WIDE, -1.0)):
        s = lax.rsqrt(dd + soften)
        s2 = s * s
        weight = (mass * s) * (s2 * sign)
        q = rw * s2
        for c in range(3):
            acc[c] = acc[c] + weight * r[c]
            acc[3 + c] = acc[3 + c] + weight * (w[c] - q * r[c])
    return tuple(acc)


def zeros():
    return tuple(jnp.zeros((8, 128), F32) for _ in range(6))


BLOCK, PLACE, LEVEL, SHARD, ROW, HERE, COUNT = range(7)


def fill_slots(lev, top, cap, plan):
    for s in range(cap):
        plan[BLOCK, s] = 0
        plan[PLACE, s] = -1000
        plan[LEVEL, s] = 0
    count = jnp.int32(0)
    for group in ((2,), (0, 1)) if top == 2 else ((0, 1),):
        ones = [jnp.int32(0), jnp.int32(4)]
        for k in range(NB):
            level = lev[k]
            place = jnp.where(level == 0, ones[0], jnp.where(level == 1, ones[1], -1000))
            live = (level == 2) if group == (2,) else level <= min(top, 1)
            plan[BLOCK, count] = k
            plan[PLACE, count] = jnp.where(live, place, -1000)
            plan[LEVEL, count] = jnp.where(live, level, 0)
            count = count + live.astype(jnp.int32)
            ones[0] = ones[0] + (level == 0).astype(jnp.int32)
            ones[1] = ones[1] + (level == 1).astype(jnp.int32)
        if group == (2,):
            plan[COUNT, 2] = count
    plan[COUNT, 0] = count
    plan[COUNT, 3] = ones[0]


def fill_near(plan, cap, own, levall, partner, sent):
    def slot(s, _):
        k = plan[BLOCK, s]
        q = partner[k] // NB
        level = levall[q, k]
        place = jnp.where(level == 0, 0, 4)
        for e in range(NB):
            place = place + ((levall[q, e] == level) & (e < k)).astype(jnp.int32)
        ours = plan[LEVEL, s] <= sent
        theirs = (q != own) & (level <= sent)
        for e, (b, row, here) in enumerate(((own, plan[PLACE, s], ours), (q, place, theirs))):
            plan[SHARD, 2 * s + e] = b
            plan[ROW, 2 * s + e] = jnp.clip(jnp.where(here, row, 0), 0, 3 if sent == 0 else 7)
            plan[HERE, 2 * s + e] = here.astype(jnp.int32)
        return 0

    lax.fori_loop(0, cap, slot, 0)


def span_of(level):
    return jnp.where(level == 0, TICK, jnp.where(level == 1, 2 * TICK, 4 * TICK)).astype(F32)


XS, MS, VS, AS, JS = (0, 1, 2), 3, (4, 5, 6), (8, 9, 10), (11, 12, 13)


def columns(tile):
    return tuple(
        [tile[:, c : c + 1] for c in group] for group in (XS, VS, AS, JS)
    )


def forecast(x, v, a, j, t):
    t2 = t * t * 0.5
    t3 = t * t * t * (1.0 / 6.0)
    xp = [x[c] + v[c] * t + a[c] * t2 + j[c] * t3 for c in range(3)]
    vp = [v[c] + a[c] * t + j[c] * t2 for c in range(3)]
    return xp + vp


QUANTITIES = 7


def fill_sources(table, rates, predicted, t):
    t2 = t * t * 0.5
    t3 = t * t * t / 6.0

    def shard(b, _):
        x, m, v = [[table[b, pl.ds(NB * f, NB), :] for f in group] for group in ((0, 1, 2), (3,), (4, 5, 6))]
        a, j = [[rates[b, pl.ds(NB * f, NB), :] for f in group] for group in ((0, 1, 2), (3, 4, 5))]
        for c in range(3):
            predicted[b, c] = x[c] + v[c] * t + a[c] * t2 + j[c] * t3
            predicted[b, 4 + c] = v[c] + a[c] * t + j[c] * t2
        predicted[b, 3] = m[0]
        return 0

    lax.fori_loop(0, table.shape[0], shard, 0)
    for f in range(QUANTITIES):
        predicted[table.shape[0], f] = jnp.zeros((NB, BS), F32)


def target_of(state, plan, s):
    x, v, a, j = columns(state[plan[BLOCK, s]])
    ahead = forecast(x, v, a, j, span_of(plan[LEVEL, s]))
    return [jnp.broadcast_to(value, (8, 128)) for value in ahead]


def broad(row):
    return jnp.broadcast_to(row, (8, 128))


def tile_rows(tile):
    return [broad(tile(r)) for r in (0, 1, 2, 4, 5, 6)], broad(tile(3))


def from_table(table, b, k):
    return tile_rows(lambda r: table[b, pl.ds(NB * r + k, 1), :])


def from_predicted(predicted, b, k):
    return tile_rows(lambda r: predicted[b, r, pl.ds(k, 1), :])


def slot_pairs(first, last, state, plan, sweep, prepare, close, sink, carry):
    def two(p, carry):
        goal = [target_of(state, plan, 2 * p + e) for e in range(2)]
        prepare(p)
        acc = sweep(goal)
        for e in range(2):
            s = 2 * p + e
            near = zeros()
            for part in range(2):
                rows, mass, wanted = close(s, e, part)
                near = pair_split(goal[e], rows, mass * jnp.where(wanted, 1.0, 0.0).astype(F32), near)
            total, inner = (
                [jnp.sum(value, axis=1, keepdims=True) for value in group] for group in (acc[e], near)
            )
            carry = sink(s, total, inner, carry)
        return carry

    return lax.fori_loop(first, last, two, carry)


def pairs_of(plan):
    return (plan[COUNT, 0] + 1) // 2


def sweep_table(groups, load):
    def sweep(goal):
        def group(b, acc):
            for k in range(NB):
                rows, mass = load(b, k)
                acc = tuple(pair(goal[e], rows, mass, WIDE, acc[e]) for e in range(2))
            return acc

        return lax.fori_loop(0, groups, group, (zeros(), zeros()))

    return sweep


def fill_received(got, turned):
    senders, _, lanes = got.shape
    for t in range(lanes // 128):
        for half in range(senders // 128):
            part = got[pl.ds(half * 128, 128), 0, pl.ds(t * 128, 128)]
            turned[pl.ds(t * 16, 16), :, pl.ds(half * 128, 128)] = part.T.reshape(16, 8, 128)


def sweep_received(turned, mass, slots_in, used):
    def sweep(goal):
        def slot(s, acc):
            for i in range(8):
                for half in range(turned.shape[2] // 128):
                    at = pl.ds(half * 128, 128)
                    rows = [broad(turned[f * slots_in + s, i : i + 1, at]) for f in range(6)]
                    m = broad(mass[s, i : i + 1, at])
                    acc = tuple(pair(goal[e], rows, m, WIDE, acc[e]) for e in range(2))
            return acc

        return lax.fori_loop(0, used, slot, (zeros(), zeros()))

    return sweep


def gather_blocks(turned, mass, slots_in, plan, near, p):
    lane = lax.broadcasted_iota(jnp.int32, (8, 128), 1)
    row = lax.broadcasted_iota(jnp.int32, (8, 128), 0)
    keep = lane // 16 == row
    for item in range(4):
        b = plan[SHARD, 4 * p + item]
        place = plan[ROW, 4 * p + item]
        half = pl.ds(pl.multiple_of((b // 8) * 128, 128), 128)
        shift = lax.rem(128 - lax.rem(b, 8) * 16, 128)
        for r, f in ((0, 0), (1, 1), (2, 2), (4, 3), (5, 4), (6, 5), (3, None)):
            tile = mass[place, :, half] if f is None else turned[f * slots_in + place, :, half]
            tile = pltpu.roll(pltpu.roll(tile, shift, 1), 0, 1, stride=16, stride_axis=0)
            near[item, r : r + 1, :] = jnp.sum(jnp.where(keep, tile, 0.0), axis=0, keepdims=True)


def fill_tiles(parts, tiles, width):
    per = 128 // width
    tiles = list(tiles)
    lane = lax.broadcasted_iota(jnp.int32, (8, 128), 1)
    for f, slot, column in parts:
        t = f // per
        tiles[t] = jnp.where(lane == (f % per) * width + slot * 8, column, tiles[t])
    return tiles


def blank(count):
    return [jnp.zeros((8, 128), F32) for _ in range(count)]


def place_tiles(tiles):
    tiles = [pltpu.roll(tile, 0, 1, stride=1, stride_axis=0) for tile in tiles]
    return [jnp.sum(tile, axis=0, keepdims=True) for tile in tiles]


def send(tiles, pay):
    for t, tile in enumerate(tiles):
        full = jnp.broadcast_to(tile[None], (pay.shape[0], 1, 128))
        pay[:, :, pl.ds(t * 128, 128)] = full


def corrector(step, state, plan, sums):
    lane = lax.broadcasted_iota(jnp.int32, (8, 128), 1)

    def sink(s, total, inner, carry):
        k = plan[BLOCK, s]
        t = span_of(plan[LEVEL, s])
        tile = state[k]
        x, v, a, j = columns(tile)
        if sums is not None:
            before = sums[s]
            total = [total[c] + before[:, c : c + 1] for c in range(6)]
            inner = [inner[c] + before[:, 8 + c : 9 + c] for c in range(6)]
        total = [total[c] + inner[c] for c in range(6)]
        half = t * 0.5
        twelfth = t * t * (1.0 / 12.0)
        v1 = [v[c] + (a[c] + total[c]) * half + (j[c] - total[3 + c]) * twelfth for c in range(3)]
        x1 = [x[c] + (v[c] + v1[c]) * half + (a[c] - total[c]) * twelfth for c in range(3)]
        if step == 3:
            parts = [(f, s, column) for f, column in enumerate(x1 + v1 + total + inner)]
            return tuple(fill_tiles(parts, carry, 64))
        fresh = tile
        for at, column in zip(XS + VS + AS + JS, x1 + v1 + total):
            fresh = jnp.where(lane == at, column, fresh)
        state[jnp.where(s < plan[COUNT, 0], k, NB)] = fresh
        ahead = forecast(x1, v1, total[:3], total[3:], TICK)
        if step == 0:
            ahead = ahead + [tile[:, MS : MS + 1]]
        parts = [(f, plan[PLACE, s], column) for f, column in enumerate(ahead)]
        return tuple(fill_tiles(parts, carry, 32 if step == 0 else 64))

    return sink


def fill_later(state, lev, later):
    parts = []
    seen = jnp.int32(4)
    for k in range(NB):
        one = lev[k] == 1
        mark = jnp.where(one, seen, -1000)
        x, v, a, j = columns(state[k])
        for f, column in enumerate(forecast(x, v, a, j, 2 * TICK)):
            parts.append((f, mark, column))
        seen = seen + one.astype(jnp.int32)
    for t, tile in enumerate(fill_tiles(parts, blank(3), 64)):
        later[t] = tile


def pack_kernel(ps, fr, mass, lev, first, rates, own):
    x, v, a, j = ps[0:3, :], ps[3:6, :], fr[0:3, :], fr[3:6, :]
    t2 = TICK * TICK * 0.5
    xp = x + v * TICK + a * t2 + j * (TICK * TICK * TICK / 6.0)
    vp = v + a * TICK + j * t2
    ap = a + j * TICK
    lane = lax.broadcasted_iota(jnp.int32, (8, BS), 1)
    levels = jnp.zeros((8, BS), F32)
    for k in range(NB):
        levels = jnp.where(lane == k, lev[k].astype(F32), levels)
    first[7 * NB : 7 * NB + 8, :] = levels
    for k in range(NB):
        at = slice(k * BS, k * BS + BS)
        for c in range(3):
            first[NB * c + k : NB * c + k + 1, :] = xp[c : c + 1, at]
            first[NB * (4 + c) + k : NB * (4 + c) + k + 1, :] = vp[c : c + 1, at]
            rates[0, NB * c + k : NB * c + k + 1, :] = ap[c : c + 1, at]
            rates[0, NB * (3 + c) + k : NB * (3 + c) + k + 1, :] = j[c : c + 1, at]
        first[NB * 3 + k : NB * 3 + k + 1, :] = mass[:, at]
        own[k] = jnp.zeros((16, BS), F32)
        own[k, 0:3, :] = x[:, at]
        own[k, 3:4, :] = mass[:, at]
        own[k, 4:7, :] = v[:, at]
        own[k, 8:14, :] = fr[:, at]
    for b in range(1, rates.shape[0]):
        rates[b] = rates[0]


def first_kernel(me, col, table, mine, lev, levall, partner, state, pay, order0, order1, turned, plan):
    me = me[0]
    col = pl.multiple_of(col[0] * 8, 8)
    fill_slots(lev, TOP[0], CAPS[0], plan)
    for k in range(NB):
        turned[k, :, 0:16] = mine[k].T
    for k in range(NB):
        state[k] = turned[k, pl.ds(col, 8), :]
    masses = []
    seen = jnp.int32(0)
    for k in range(NB):
        one = lev[k] == 1
        masses.append((7, jnp.where(one, seen, -1000), state[k][:, MS : MS + 1]))
        seen = seen + one.astype(jnp.int32)

    def close(s, e, part):
        k = plan[BLOCK, s]
        b = partner[k] // NB if part else me
        rows, mass = from_table(table, b, k)
        return rows, mass, b != me if part else jnp.bool_(True)

    shards = table.shape[0]
    orders = (order0, order1)

    def sweep(goal):
        def group(b, carry):
            acc, counts = carry
            for k in range(NB):
                rows, mass = from_table(table, b, k)
                acc = tuple(pair(goal[e], rows, mass, WIDE, acc[e]) for e in range(2))
                for order, count in zip(orders, counts):
                    order[count] = b * NB + k
                counts = tuple(counts[e] + (levall[b, k] > e).astype(jnp.int32) for e in range(2))
            return acc, counts

        start = ((zeros(), zeros()), (jnp.int32(0), jnp.int32(0)))
        acc, counts = lax.fori_loop(0, shards, group, start)
        for order, count in zip(orders, counts):
            for e in range(NB):
                order[count + e] = shards * NB
            order[(shards + 2) * NB] = count
        return acc

    tiles = slot_pairs(
        0, pairs_of(plan), state, plan, sweep,
        lambda p: None, close, corrector(0, state, plan, None),
        tuple(fill_tiles(masses, blank(2), 32)),
    )
    send(place_tiles(tiles), pay)


def ahead_sums(step, first, last, me, plan, order, predicted, state, sums):
    lane = lax.broadcasted_iota(jnp.int32, (8, 128), 1)

    def load(g, e):
        index = order[g * NB + e]
        return from_predicted(predicted, index // NB, lax.rem(index, NB))

    def close(s, e, part):
        rows, mass = from_predicted(predicted, plan[SHARD, 2 * s + part], plan[BLOCK, s])
        other = plan[SHARD, 2 * s + 1] != me if part else jnp.bool_(True)
        return rows, mass, other & (plan[HERE, 2 * s + part] == 0)

    def sink(s, total, inner, carry):
        tile = jnp.zeros((8, 128), F32)
        for at, group in ((0, total), (8, inner)):
            for c in range(6):
                tile = jnp.where(lane == at + c, group[c], tile)
        sums[s] = tile
        return carry

    groups = (order[order.shape[0] - NB] + NB - 1) // NB
    slot_pairs(first, last, state, plan, sweep_table(groups, load), lambda p: None, close, sink, 0)


def early_pairs(plan):
    return jnp.where((plan[COUNT, 2] >= 2) & (plan[COUNT, 3] <= 2), 1, 0)


def ahead_kernel(step, me, table, rates, lev, levall, partner, order, state, *rest):
    if step == 1:
        sums, plan, predicted = rest
    elif step == 2:
        sums, plan, later, early, predicted, plan3 = rest
    else:
        early, sums, plan, predicted = rest
    me = me[0]
    fill_slots(lev, TOP[step], CAPS[step], plan)
    fill_near(plan, CAPS[step], me, levall, partner, SENT[step])
    fill_sources(table, rates, predicted, step * TICK)
    first = 0
    if step == 3:
        first = early_pairs(plan)
        sums[0:2] = early[...]
    ahead_sums(step, first, pairs_of(plan), me, plan, order, predicted, state, sums)
    if step == 2:
        fill_later(state, lev, later)
        fill_slots(lev, TOP[3], CAPS[3], plan3)
        fill_near(plan3, 2, me, levall, partner, SENT[3])
        fill_sources(table, rates, predicted, 3 * TICK)
        early[...] = jnp.zeros((2, 8, 128), F32)
        ahead_sums(3, 0, early_pairs(plan3), me, plan3, order, predicted, state, early)
    if step == 1:
        level = table[:, 7 * NB, :]
        lane = lax.broadcasted_iota(jnp.int32, level.shape, 1)
        one = jnp.where((level == 1.0) & (lane < NB), 1.0, 0.0).astype(F32)
        plan[COUNT, 1] = jnp.max(jnp.sum(one, axis=1, keepdims=True)).astype(jnp.int32)


def after_kernel(step, got, state_in, sums, plan, *rest):
    later = None
    used = SLOTS[step]
    if step > 1:
        masses, before, *rest = rest
        used = jnp.minimum(4 + before[COUNT, 1], used)
    if step == 2:
        later, *rest = rest
    if step == 3:
        state = state_in
    else:
        state, *rest = rest
    pay, *rest = rest
    if step == 1:
        masses, *rest = rest
    near, turned = rest
    if step < 3:
        state[...] = state_in[...]
    fill_received(got, turned)
    if step == 1:
        masses[0:4] = turned[24:28]
        masses[4:8] = turned[28:32]

    def close(s, e, part):
        rows, mass = tile_rows(lambda r: near[2 * e + part, r : r + 1, :])
        return rows, mass, plan[HERE, 2 * s + part] == 1

    tiles = slot_pairs(
        0, pairs_of(plan), state, plan,
        sweep_received(turned, masses, SLOTS[step], used),
        lambda p: gather_blocks(turned, masses, SLOTS[step], plan, near, p),
        close, corrector(step, state, plan, sums),
        tuple([later[t] for t in range(3)] if step == 2 else blank(9 if step == 3 else 3)),
    )
    send(place_tiles(tiles), pay)


def last_kernel(got, ps, fr, irr, plan, kin, comb, close):
    count = plan[COUNT, 0]
    kin[...] = ps[...]
    comb[...] = fr[...]
    close[...] = irr[...]
    senders = got.shape[0]
    lane = lax.broadcasted_iota(jnp.int32, (senders, 128), 1)
    row = lax.broadcasted_iota(jnp.int32, (senders, 128), 0)
    spread = [pltpu.roll(got[:, 0, pl.ds(t * 128, 128)], 0, 1, stride=8, stride_axis=0) for t in range(9)]
    place = lane - row * 8

    def slot(s, _):
        at = pl.ds(pl.multiple_of(plan[BLOCK, s] * BS, BS), BS)
        for f in range(18):
            t, e = divmod(f, 2)
            start = e * 64 + s * 8
            keep = (((place - start) & 127) >> 3) == 0
            value = jnp.sum(jnp.where(keep, spread[t], 0.0), axis=0, keepdims=True)
            out = (kin, comb, close)[f // 6]
            out[f % 6 : f % 6 + 1, at] = pltpu.roll(value, (128 - start) & 127, 1)
        return 0

    lax.fori_loop(0, count, slot, 0)


def body(phase_space, force_rates, irregular, stellar_masses, levels, active, partner):
    shards = lax.axis_size("blk")
    columns_ = lax.axis_size("grp")
    everyone = shards * columns_
    me = lax.axis_index("blk").astype(jnp.int32).reshape(1)
    col = lax.axis_index("grp").astype(jnp.int32).reshape(1)
    tiles = lambda count: pltpu.VMEM((count, 8, 128), F32)
    array = lambda *shape: jax.ShapeDtypeStruct(shape, F32)
    near = lambda *shape: pltpu.VMEM(shape, F32)
    here = lambda x: pltpu.with_memory_space_constraint(x, pltpu.VMEM)
    plan_shape = jax.ShapeDtypeStruct((8, 32), jnp.int32)
    state_shape = near(NB + 1, 8, 128)

    def exchange(pay, axis):
        return lax.all_to_all(pay, axis, split_axis=0, concat_axis=0, tiled=True)

    packed, rates, mine = pl.pallas_call(
        pack_kernel,
        out_shape=(array(7 * NB + 8, BS), array(shards, 6 * NB, BS), near(NB, 16, BS)),
        in_specs=[VMEM, VMEM, VMEM, SMEM],
        out_specs=(VMEM, VMEM, VMEM),
        name="pack",
    )(phase_space, force_rates, stellar_masses[None, :], levels)
    table = lax.all_gather(packed, "blk", axis=0, tiled=False)
    levall = table[:, 7 * NB, :NB].astype(jnp.int32)
    table, rates = lax.optimization_barrier((table, rates))
    rates = exchange(rates, "blk")
    order_shape = jax.ShapeDtypeStruct(((shards + 3) * NB,), jnp.int32)
    state, pay, *orders = pl.pallas_call(
        first_kernel,
        out_shape=(state_shape, array(everyone, 1, 256), order_shape, order_shape),
        in_specs=[SMEM, SMEM, VMEM, VMEM, SMEM, SMEM, SMEM],
        out_specs=(VMEM, VMEM, SMEM, SMEM),
        scratch_shapes=[pltpu.VMEM((NB, 128, 128), F32), pltpu.SMEM((8, 32), jnp.int32)],
        name="first",
    )(me, col, here(table), here(mine), levels, levall, partner)
    masses = before = None
    for step in (1, 2, 3):
        cap = CAPS[step]
        lanes = (0, 256, 384, 384)[step]
        got = exchange(pay, ("blk", "grp"))
        ins = (me, here(table), here(rates), levels, levall, partner, orders[SENT[step]], here(state))
        specs = [SMEM, VMEM, VMEM, SMEM, SMEM, SMEM, SMEM, VMEM]
        out_shape = (near(cap, 8, 128), plan_shape)
        out_specs = (VMEM, SMEM)
        scratch = [pltpu.VMEM((shards + 1, QUANTITIES, NB, BS), F32)]
        if step == 2:
            out_shape += (near(3, 8, 128), near(2, 8, 128))
            out_specs += (VMEM, VMEM)
            scratch += [pltpu.SMEM((8, 32), jnp.int32)]
        elif step == 3:
            ins += (here(early),)
            specs += [VMEM]
        outs = pl.pallas_call(
            functools.partial(ahead_kernel, step),
            out_shape=out_shape,
            in_specs=specs,
            out_specs=out_specs,
            scratch_shapes=scratch,
            name=f"ahead{step}",
        )(*ins)
        sums, plan = outs[:2]
        if step == 2:
            early = outs[3]
        ins = (here(got), here(state), here(sums), plan)
        specs = [VMEM, VMEM, VMEM, SMEM]
        if step > 1:
            ins += (here(masses), before)
            specs += [VMEM, SMEM]
        if step == 2:
            ins += (here(outs[2]),)
            specs += [VMEM]
        pay_shape = array(everyone if step < 3 else columns_, 1, (0, 384, 384, 1152)[step])
        out_shape = {
            1: (state_shape, pay_shape, near(8, 8, everyone)), 2: (state_shape, pay_shape), 3: (pay_shape,),
        }[step]
        outs = pl.pallas_call(
            functools.partial(after_kernel, step),
            out_shape=out_shape,
            in_specs=specs,
            out_specs=tuple(VMEM for _ in out_shape),
            scratch_shapes=[
                tiles(4),
                pltpu.VMEM((lanes // 8, 8, everyone), F32),
            ],
            name=f"after{step}",
        )(*ins)
        if step == 1:
            state, pay, masses = outs
            before = plan
        elif step == 2:
            state, pay = outs
        else:
            (pay,) = outs
    got = exchange(pay, "grp")
    shape = array(6, W)
    return tuple(
        pl.pallas_call(
            last_kernel,
            out_shape=(shape, shape, shape),
            in_specs=[VMEM, VMEM, VMEM, VMEM, SMEM],
            out_specs=(VMEM, VMEM, VMEM),
            name="last",
        )(here(got), phase_space, force_rates, irregular, plan)
    )


def solution(mesh):
    in_specs = (
        P(None, "blk"), P(None, "blk"), P(None, "blk"), P("blk"), P("blk"), P(None, "blk"), P("blk"),
    )
    out_specs = (P(None, "blk"), P(None, "blk"), P(None, "blk"))
    return jax.shard_map(body, mesh=mesh, in_specs=in_specs, out_specs=out_specs, check_vma=False)
```

profile of v0, /device:TPU:1, one launch (start us, length us, event | category | flops | bytes accessed | tf_op | source)
XLA Modules:
  0.0 158.3 jit_solution(4335389193097675667)
XLA Ops:
  0.6 2.0 %pack.1 = (f32[120,128]{1,0:T(8,128)}, f32[16,96,128]{2,1,0:T(8,128)}, f32[16,16,128]{2,1,0:T(8,128)S(1)}) custom-call(f32[6,2048]{1,0:T(8,128)} %ps.3, f32[6,2048]{1,0:T(8,128)} %fr.3, f32[1,2048]{1,0:T(1,128)} %bitcast.13, s32[16]{0:T(128)} %lev.9), custom_call_target="tpu_custom_call" | custom-call | tf_op jit(solution)/shard_map/pack/pallas_call | solution.py:534
  2.6 24.2 %all-gather = f32[1920,128]{1,0:T(8,128)S(1)} all-gather(f32[120,128]{1,0:T(8,128)} %get-tuple-element.25), channel_id=2, replica_groups=mesh['blk'=16,'grp'=16] {'blk'}, dimensions={0}, use_global_device_ids=true | all-gather | bytes 1044480 | tf_op jit(solution)/shard_map/all_gather | solution.py:541
  26.7 3.6 %all-to-all-start.1 = ((f32[16,96,128]{2,1,0:T(8,128)}), f32[16,96,128]{2,1,0:T(8,128)S(1)}, u32[]{:S(2)}, u32[]{:S(2)}) async-start(f32[16,96,128]{2,1,0:T(8,128)} %get-tuple-element.31), calls=%async_computation.1 | async-start | bytes 1572864 | tf_op jit(solution)/shard_map/all_to_all | solution.py:532
  30.3 0.6 convert_bitcast_fusion.levall
  30.9 6.0 %first.1 = (f32[17,8,128]{2,1,0:T(8,128)S(1)}, f32[256,1,256]{2,1,0:T(1,128)}, s32[304]{0:T(512)}, s32[304]{0:T(512)}) custom-call(s32[1]{0:T(128)} %bitcast.me, s32[1]{0:T(128)} %bitcast.1.col, f32[16,120,128]{2,1,0:T(8,128)S(1)} %bitcast.8, f32[16,16,128]{2,1,0:T(8,128)S(1)} %get-tuple-element.28.mine, s32[16]{0:T(128)} %lev.9, ...), custom_call_target="tpu_custom_call" | custom-call | tf_op jit(solution)/shard_map/first/pallas_call | solution.py:546
  36.9 5.6 %all-to-all-done.1.rates = f32[16,96,128]{2,1,0:T(8,128)S(1)} async-done(((f32[16,96,128]{2,1,0:T(8,128)}), f32[16,96,128]{2,1,0:T(8,128)S(1)}, u32[]{:S(2)}, u32[]{:S(2)}) %all-to-all-start.1) | async-done | bytes 786464 | tf_op jit(solution)/shard_map/all_to_all | solution.py:532
  42.5 0.0 copy-start
  42.5 13.4 %all-to-all-start = ((f32[256,1,256]{2,1,0:T(1,128)}), f32[256,1,256]{2,1,0:T(1,128)S(1)}, u32[]{:S(2)}, u32[]{:S(2)}) async-start(f32[256,1,256]{2,1,0:T(1,128)} %get-tuple-element.29), calls=%async_computation | async-start | bytes 524288 | tf_op jit(solution)/shard_map/all_to_all | solution.py:532
  55.9 8.3 %ahead1.1 = (f32[6,8,128]{2,1,0:T(8,128)S(1)}, s32[8,32]{1,0:T(8,128)}) custom-call(s32[1]{0:T(128)} %bitcast.me, f32[16,120,128]{2,1,0:T(8,128)S(1)} %bitcast.9, f32[16,96,128]{2,1,0:T(8,128)S(1)} %all-to-all-done.1.rates, s32[16]{0:T(128)} %lev.9, s32[16,16]{1,0:T(8,128)} %convert_bitcast_fusion.levall, s32[16]{0:T(128)} %partner.7, ...), custom_call_target="tpu_custom_call" | custom-call | tf_op jit(solution)/shard_map/ahead1/pallas_call | solution.py:571
  64.2 0.0 copy-done
  64.2 7.3 %all-to-all-done.got = f32[256,1,256]{2,1,0:T(1,128)S(1)} async-done(((f32[256,1,256]{2,1,0:T(1,128)}), f32[256,1,256]{2,1,0:T(1,128)S(1)}, u32[]{:S(2)}, u32[]{:S(2)}) %all-to-all-start) | async-done | bytes 262176 | tf_op jit(solution)/shard_map/all_to_all | solution.py:532
  71.5 0.0 copy-start.1
  71.5 5.4 %after1.1 = (f32[17,8,128]{2,1,0:T(8,128)S(1)}, f32[256,1,384]{2,1,0:T(1,128)}, f32[8,8,256]{2,1,0:T(8,128)S(1)}) custom-call(f32[256,1,256]{2,1,0:T(1,128)S(1)} %all-to-all-done.got, f32[17,8,128]{2,1,0:T(8,128)S(1)} %get-tuple-element.30.state.state_in, f32[6,8,128]{2,1,0:T(8,128)S(1)} %get-tuple-element.33.sums, s32[8,32]{1,0:T(8,128)} %get-tuple-element.34.plan.rest_1_), custom_call_target="tpu_custom_call" | custom-call | tf_op jit(solution)/shard_map/after1/pallas_call | solution.py:594
  76.9 10.8 %all-to-all-start.2 = ((f32[256,1,384]{2,1,0:T(1,128)}), f32[256,1,384]{2,1,0:T(1,128)S(1)}, u32[]{:S(2)}, u32[]{:S(2)}) async-start(f32[256,1,384]{2,1,0:T(1,128)} %get-tuple-element.35), calls=%async_computation.2 | async-start | bytes 786432 | tf_op jit(solution)/shard_map/all_to_all | solution.py:532
  87.8 0.0 copy-done.1
  87.8 8.5 %ahead2.1 = (f32[4,8,128]{2,1,0:T(8,128)S(1)}, s32[8,32]{1,0:T(8,128)}, f32[3,8,128]{2,1,0:T(8,128)S(1)}, f32[2,8,128]{2,1,0:T(8,128)S(1)}) custom-call(s32[1]{0:T(128)} %bitcast.me, f32[16,120,128]{2,1,0:T(8,128)S(1)} %bitcast.10, f32[16,96,128]{2,1,0:T(8,128)S(1)} %copy-done.1, s32[16]{0:T(128)} %lev.9, s32[16,16]{1,0:T(8,128)} %convert_bitcast_fusion.levall, ...), custom_call_target="tpu_custom_call" | custom-call | tf_op jit(solution)/shard_map/ahead2/pallas_call | solution.py:571
  96.2 0.0 copy-start.2
  96.3 9.8 %all-to-all-done.2.got = f32[256,1,384]{2,1,0:T(1,128)S(1)} async-done(((f32[256,1,384]{2,1,0:T(1,128)}), f32[256,1,384]{2,1,0:T(1,128)S(1)}, u32[]{:S(2)}, u32[]{:S(2)}) %all-to-all-start.2) | async-done | bytes 393248 | tf_op jit(solution)/shard_map/all_to_all | solution.py:532
  106.1 4.1 %after2.1 = (f32[17,8,128]{2,1,0:T(8,128)S(1)}, f32[256,1,384]{2,1,0:T(1,128)}) custom-call(f32[256,1,384]{2,1,0:T(1,128)S(1)} %all-to-all-done.2.got, f32[17,8,128]{2,1,0:T(8,128)S(1)} %get-tuple-element.36.state.state_in, f32[4,8,128]{2,1,0:T(8,128)S(1)} %get-tuple-element.38.sums, s32[8,32]{1,0:T(8,128)} %get-tuple-element.39.plan, ...), custom_call_target="tpu_custom_call" | custom-call | tf_op jit(solution)/shard_map/after2/pallas_call | solution.py:594
  110.2 7.0 %all-to-all-start.3 = ((f32[256,1,384]{2,1,0:T(1,128)}), f32[256,1,384]{2,1,0:T(1,128)S(1)}, u32[]{:S(2)}, u32[]{:S(2)}) async-start(f32[256,1,384]{2,1,0:T(1,128)} %get-tuple-element.42), calls=%async_computation.3 | async-start | bytes 786432 | tf_op jit(solution)/shard_map/all_to_all | solution.py:532
  117.2 0.0 copy-done.2
  117.2 8.0 %ahead3.1 = (f32[8,8,128]{2,1,0:T(8,128)S(1)}, s32[8,32]{1,0:T(8,128)}) custom-call(s32[1]{0:T(128)} %bitcast.me, f32[16,120,128]{2,1,0:T(8,128)S(1)} %bitcast.11, f32[16,96,128]{2,1,0:T(8,128)S(1)} %copy-done.2, s32[16]{0:T(128)} %lev.9, s32[16,16]{1,0:T(8,128)} %convert_bitcast_fusion.levall, s32[16]{0:T(128)} %partner.7, s32[304]{0:T(512)} %get-tuple-element.37.order, ...), custom_call_target="tpu_custom_call" | custom-call | tf_op jit(solution)/shard_map/ahead3/pallas_call | solution.py:571
  125.2 10.3 %all-to-all-done.3.got = f32[256,1,384]{2,1,0:T(1,128)S(1)} async-done(((f32[256,1,384]{2,1,0:T(1,128)}), f32[256,1,384]{2,1,0:T(1,128)S(1)}, u32[]{:S(2)}, u32[]{:S(2)}) %all-to-all-start.3) | async-done | bytes 393248 | tf_op jit(solution)/shard_map/all_to_all | solution.py:532
  135.5 7.2 %after3.1 = f32[16,1,1152]{2,1,0:T(1,128)} custom-call(f32[256,1,384]{2,1,0:T(1,128)S(1)} %all-to-all-done.3.got, f32[17,8,128]{2,1,0:T(8,128)S(1)} %get-tuple-element.43.state.state_in, f32[8,8,128]{2,1,0:T(8,128)S(1)} %get-tuple-element.45.sums, s32[8,32]{1,0:T(8,128)} %get-tuple-element.46.plan, f32[8,8,256]{2,1,0:T(8,128)S(1)} %get-tuple-element.40.rest_0_, ...), custom_call_target="tpu_custom_call" | custom-call | tf_op jit(solution)/shard_map/after3/pallas_call | solution.py:594
  142.7 13.4 %all_to_all.25.got = f32[16,1,1152]{2,1,0:T(1,128)S(1)} all-to-all(f32[16,1,1152]{2,1,0:T(1,128)} %after3.1), channel_id=1, replica_groups=mesh['blk'=16,'grp'=16] {'grp'}, dimensions={0} | all-to-all | bytes 147456 | tf_op jit(solution)/shard_map/all_to_all | solution.py:532
  156.1 2.2 %last.1 = (f32[6,2048]{1,0:T(8,128)}, f32[6,2048]{1,0:T(8,128)}, f32[6,2048]{1,0:T(8,128)}) custom-call(f32[16,1,1152]{2,1,0:T(1,128)S(1)} %all_to_all.25.got, f32[6,2048]{1,0:T(8,128)} %ps.3, f32[6,2048]{1,0:T(8,128)} %fr.3, f32[6,2048]{1,0:T(8,128)} %irr.1, s32[8,32]{1,0:T(8,128)} %get-tuple-element.46.plan), custom_call_target="tpu_custom_call" | custom-call | tf_op jit(solution)/shard_map/last/pallas_call | solution.py:615
  (1 shorter events, 0.0 us)
Async XLA Ops:
  26.7 15.8 %all-to-all-start.1 = ((f32[16,96,128]{2,1,0:T(8,128)}), f32[16,96,128]{2,1,0:T(8,128)S(1)}, u32[]{:S(2)}, u32[]{:S(2)}) async-start(f32[16,96,128]{2,1,0:T(8,128)} %get-tuple-element.31), calls=%async_computation.1 | async-start | bytes 1572864 | tf_op jit(solution)/shard_map/all_to_all | solution.py:532
  42.5 21.7 %copy-start = (f32[16,96,128]{2,1,0:T(8,128)}, f32[16,96,128]{2,1,0:T(8,128)S(1)}, u32[]{:S(2)}) copy-start(f32[16,96,128]{2,1,0:T(8,128)S(1)} %all-to-all-done.1.rates) | copy-start | bytes 2359300
  42.5 29.0 %all-to-all-start = ((f32[256,1,256]{2,1,0:T(1,128)}), f32[256,1,256]{2,1,0:T(1,128)S(1)}, u32[]{:S(2)}, u32[]{:S(2)}) async-start(f32[256,1,256]{2,1,0:T(1,128)} %get-tuple-element.29), calls=%async_computation | async-start | bytes 524288 | tf_op jit(solution)/shard_map/all_to_all | solution.py:532
  71.5 16.3 %copy-start.1 = (f32[16,96,128]{2,1,0:T(8,128)S(1)}, f32[16,96,128]{2,1,0:T(8,128)}, u32[]{:S(2)}) copy-start(f32[16,96,128]{2,1,0:T(8,128)} %copy-done) | copy-start | bytes 2359300
  76.9 29.2 %all-to-all-start.2 = ((f32[256,1,384]{2,1,0:T(1,128)}), f32[256,1,384]{2,1,0:T(1,128)S(1)}, u32[]{:S(2)}, u32[]{:S(2)}) async-start(f32[256,1,384]{2,1,0:T(1,128)} %get-tuple-element.35), calls=%async_computation.2 | async-start | bytes 786432 | tf_op jit(solution)/shard_map/all_to_all | solution.py:532
  96.2 20.9 %copy-start.2 = (f32[16,96,128]{2,1,0:T(8,128)S(1)}, f32[16,96,128]{2,1,0:T(8,128)}, u32[]{:S(2)}) copy-start(f32[16,96,128]{2,1,0:T(8,128)} %copy-done) | copy-start | bytes 2359300
  110.2 25.3 %all-to-all-start.3 = ((f32[256,1,384]{2,1,0:T(1,128)}), f32[256,1,384]{2,1,0:T(1,128)S(1)}, u32[]{:S(2)}, u32[]{:S(2)}) async-start(f32[256,1,384]{2,1,0:T(1,128)} %get-tuple-element.42), calls=%async_computation.3 | async-start | bytes 786432 | tf_op jit(solution)/shard_map/all_to_all | solution.py:532
where the time goes:
time: 161 us; the launch traced here: 158 us
  Pallas kernels  51.6 us (32%)
  blocking collectives  37.6 us (23%)
  starting transfers between devices  34.8 us (22%)
  waiting for transfers between devices  33 us (20%)
    all_to_all x4, starting transfers between devices, exchange(): return lax.all_to_all(pay, axis, split_axis=0, concat_axis=0, tiled=True)  34.8 us
    all_to_all x4, waiting for transfers between devices, exchange(): return lax.all_to_all(pay, axis, split_axis=0, concat_axis=0, tiled=True)  33 us
    pallas_call x3, Pallas kernels, body(): pl.pallas_call(functools.partial(ahead_kernel, step), out_shape=out_shape...  24.8 us
    all_gather x1, blocking collectives, body(): table = lax.all_gather(packed, 'blk', axis=0, tiled=False)  24.2 us
    pallas_call x3, Pallas kernels, body(): pl.pallas_call(functools.partial(after_kernel, step), out_shape=out_shape...  16.7 us
    all_to_all x1, blocking collectives, exchange(): return lax.all_to_all(pay, axis, split_axis=0, concat_axis=0, tiled=True)  13.4 us
    pallas_call x1, Pallas kernels, body(): pl.pallas_call(first_kernel, out_shape=(state_shape, array(everyone, 1, 2...  6 us
  transfers between devices with their start and end apart: 4, of which 4 were waited for; matrix products, arithmetic and copies ran while one was open for 0% of the time, Pallas kernels for 19%

commit v1 on v0

--- a/solution.py
+++ b/solution.py
@@ -82,7 +82,6 @@
         if group == (2,):
             plan[COUNT, 2] = count
     plan[COUNT, 0] = count
-    plan[COUNT, 3] = ones[0]
 
 
 def fill_near(plan, cap, own, levall, partner, sent):
@@ -420,7 +419,7 @@
 
 
 def early_pairs(plan):
-    return jnp.where((plan[COUNT, 2] >= 2) & (plan[COUNT, 3] <= 2), 1, 0)
+    return jnp.minimum(plan[COUNT, 2] // 2, 1)
 
 
 def ahead_kernel(step, me, table, rates, lev, levall, partner, order, state, *rest):
@@ -525,7 +524,8 @@
     array = lambda *shape: jax.ShapeDtypeStruct(shape, F32)
     near = lambda *shape: pltpu.VMEM(shape, F32)
     here = lambda x: pltpu.with_memory_space_constraint(x, pltpu.VMEM)
-    plan_shape = jax.ShapeDtypeStruct((8, 32), jnp.int32)
+    kept = lambda x: pltpu.with_memory_space_constraint(x, pltpu.SMEM)
+    plan_shape = pltpu.SMEM((8, 32), jnp.int32)
     state_shape = near(NB + 1, 8, 128)
 
     def exchange(pay, axis):
@@ -542,7 +542,7 @@
     levall = table[:, 7 * NB, :NB].astype(jnp.int32)
     table, rates = lax.optimization_barrier((table, rates))
     rates = exchange(rates, "blk")
-    order_shape = jax.ShapeDtypeStruct(((shards + 3) * NB,), jnp.int32)
+    order_shape = pltpu.SMEM(((shards + 3) * NB,), jnp.int32)
     state, pay, *orders = pl.pallas_call(
         first_kernel,
         out_shape=(state_shape, array(everyone, 1, 256), order_shape, order_shape),
@@ -556,7 +556,7 @@
         cap = CAPS[step]
         lanes = (0, 256, 384, 384)[step]
         got = exchange(pay, ("blk", "grp"))
-        ins = (me, here(table), here(rates), levels, levall, partner, orders[SENT[step]], here(state))
+        ins = (me, here(table), here(rates), levels, levall, partner, kept(orders[SENT[step]]), here(state))
         specs = [SMEM, VMEM, VMEM, SMEM, SMEM, SMEM, SMEM, VMEM]
         out_shape = (near(cap, 8, 128), plan_shape)
         out_specs = (VMEM, SMEM)
@@ -579,10 +579,10 @@
         sums, plan = outs[:2]
         if step == 2:
             early = outs[3]
-        ins = (here(got), here(state), here(sums), plan)
+        ins = (here(got), here(state), here(sums), kept(plan))
         specs = [VMEM, VMEM, VMEM, SMEM]
         if step > 1:
-            ins += (here(masses), before)
+            ins += (here(masses), kept(before))
             specs += [VMEM, SMEM]
         if step == 2:
             ins += (here(outs[2]),)
@@ -618,7 +618,7 @@
             in_specs=[VMEM, VMEM, VMEM, VMEM, SMEM],
             out_specs=(VMEM, VMEM, VMEM),
             name="last",
-        )(here(got), phase_space, force_rates, irregular, plan)
+        )(here(got), phase_space, force_rates, irregular, kept(plan))
     )
 
 

time: 161 us -> 158 us (0.981)
  waiting for transfers between devices: 33 us -> 29.6 us
  Pallas kernels: 51.6 us -> 54.6 us
  starting transfers between devices: 34.8 us -> 31.9 us
    pallas_call x1, Pallas kernels: 6 us -> 9.73 us  [body(): pl.pallas_call(first_kernel, out_shape=(state_shape, array(everyone, 1, 2...]
    all_to_all x4, waiting for transfers between devices: 33 us -> 29.6 us  [exchange(): return lax.all_to_all(pay, axis, split_axis=0, concat_axis=0, tiled=True)]
    all_to_all x4, starting transfers between devices: 34.8 us -> 31.9 us  [exchange(): return lax.all_to_all(pay, axis, split_axis=0, concat_axis=0, tiled=True)]
  transfers between devices with their start and end apart: 4 -> 4, of which waited for: 4 -> 4; matrix products, arithmetic and copies ran while one was open for 0% -> 0% of each run, Pallas kernels for 19% -> 22%
where the time goes in v1:
time: 158 us; the launch traced here: 155 us
  Pallas kernels  54.6 us (35%)
  blocking collectives  37.2 us (24%)
  starting transfers between devices  31.9 us (20%)
  waiting for transfers between devices  29.6 us (19%)
    all_to_all x4, starting transfers between devices, exchange(): return lax.all_to_all(pay, axis, split_axis=0, concat_axis=0, tiled=True)  31.9 us
    all_to_all x4, waiting for transfers between devices, exchange(): return lax.all_to_all(pay, axis, split_axis=0, concat_axis=0, tiled=True)  29.6 us
    pallas_call x3, Pallas kernels, body(): pl.pallas_call(functools.partial(ahead_kernel, step), out_shape=out_shape...  24.4 us
    all_gather x1, blocking collectives, body(): table = lax.all_gather(packed, 'blk', axis=0, tiled=False)  24.2 us
    pallas_call x3, Pallas kernels, body(): pl.pallas_call(functools.partial(after_kernel, step), out_shape=out_shape...  16.3 us
    all_to_all x1, blocking collectives, exchange(): return lax.all_to_all(pay, axis, split_axis=0, concat_axis=0, tiled=True)  13 us
    pallas_call x1, Pallas kernels, body(): pl.pallas_call(first_kernel, out_shape=(state_shape, array(everyone, 1, 2...  9.73 us
  transfers between devices with their start and end apart: 4, of which 4 were waited for; matrix products, arithmetic and copies ran while one was open for 0% of the time, Pallas kernels for 22%

profile of v1, /device:TPU:1, one launch (start us, length us, event | category | flops | bytes accessed | tf_op | source)
XLA Modules:
  0.0 154.6 jit_solution(15649306060859832381)
XLA Ops:
  0.6 2.0 %pack.1 = (f32[120,128]{1,0:T(8,128)}, f32[16,96,128]{2,1,0:T(8,128)}, f32[16,16,128]{2,1,0:T(8,128)S(1)}) custom-call(f32[6,2048]{1,0:T(8,128)} %ps.3, f32[6,2048]{1,0:T(8,128)} %fr.3, f32[1,2048]{1,0:T(1,128)} %bitcast.13, s32[16]{0:T(128)} %lev.9), custom_call_target="tpu_custom_call" | custom-call | tf_op jit(solution)/shard_map/pack/pallas_call | solution.py:534
  2.6 24.2 %all-gather = f32[1920,128]{1,0:T(8,128)S(1)} all-gather(f32[120,128]{1,0:T(8,128)} %get-tuple-element.25), channel_id=2, replica_groups=mesh['blk'=16,'grp'=16] {'blk'}, dimensions={0}, use_global_device_ids=true | all-gather | bytes 1044480 | tf_op jit(solution)/shard_map/all_gather | solution.py:541
  26.7 3.6 %all-to-all-start.1 = ((f32[16,96,128]{2,1,0:T(8,128)}), f32[16,96,128]{2,1,0:T(8,128)S(1)}, u32[]{:S(2)}, u32[]{:S(2)}) async-start(f32[16,96,128]{2,1,0:T(8,128)} %get-tuple-element.31), calls=%async_computation.1 | async-start | bytes 1572864 | tf_op jit(solution)/shard_map/all_to_all | solution.py:532
  30.3 0.6 convert_bitcast_fusion.levall
  30.9 9.7 %first.1 = (f32[17,8,128]{2,1,0:T(8,128)S(1)}, f32[256,1,256]{2,1,0:T(1,128)}, s32[304]{0:T(512)S(4)}, s32[304]{0:T(512)S(4)}) custom-call(s32[1]{0:T(128)} %bitcast.me, s32[1]{0:T(128)} %bitcast.1.col, f32[16,120,128]{2,1,0:T(8,128)S(1)} %bitcast.8, f32[16,16,128]{2,1,0:T(8,128)S(1)} %get-tuple-element.28.mine, s32[16]{0:T(128)} %lev.9, ...), custom_call_target="tpu_custom_call" | custom-call | tf_op jit(solution)/shard_map/first/pallas_call | solution.py:546
  40.7 1.9 %all-to-all-done.1.rates = f32[16,96,128]{2,1,0:T(8,128)S(1)} async-done(((f32[16,96,128]{2,1,0:T(8,128)}), f32[16,96,128]{2,1,0:T(8,128)S(1)}, u32[]{:S(2)}, u32[]{:S(2)}) %all-to-all-start.1) | async-done | bytes 786464 | tf_op jit(solution)/shard_map/all_to_all | solution.py:532
  42.5 0.0 copy-start
  42.5 13.4 %all-to-all-start = ((f32[256,1,256]{2,1,0:T(1,128)}), f32[256,1,256]{2,1,0:T(1,128)S(1)}, u32[]{:S(2)}, u32[]{:S(2)}) async-start(f32[256,1,256]{2,1,0:T(1,128)} %get-tuple-element.29), calls=%async_computation | async-start | bytes 524288 | tf_op jit(solution)/shard_map/all_to_all | solution.py:532
  55.9 7.3 %ahead1.1 = (f32[6,8,128]{2,1,0:T(8,128)S(1)}, s32[8,32]{1,0:T(8,128)S(4)}) custom-call(s32[1]{0:T(128)} %bitcast.me, f32[16,120,128]{2,1,0:T(8,128)S(1)} %bitcast.9, f32[16,96,128]{2,1,0:T(8,128)S(1)} %all-to-all-done.1.rates, s32[16]{0:T(128)} %lev.9, s32[16,16]{1,0:T(8,128)} %convert_bitcast_fusion.levall, s32[16]{0:T(128)} %partner.7, ...), custom_call_target="tpu_custom_call" | custom-call | tf_op jit(solution)/shard_map/ahead1/pallas_call | solution.py:571
  63.2 0.0 copy-done
  63.2 8.3 %all-to-all-done.got = f32[256,1,256]{2,1,0:T(1,128)S(1)} async-done(((f32[256,1,256]{2,1,0:T(1,128)}), f32[256,1,256]{2,1,0:T(1,128)S(1)}, u32[]{:S(2)}, u32[]{:S(2)}) %all-to-all-start) | async-done | bytes 262176 | tf_op jit(solution)/shard_map/all_to_all | solution.py:532
  71.5 0.0 copy-start.1
  71.5 4.6 %after1.1 = (f32[17,8,128]{2,1,0:T(8,128)S(1)}, f32[256,1,384]{2,1,0:T(1,128)}, f32[8,8,256]{2,1,0:T(8,128)S(1)}) custom-call(f32[256,1,256]{2,1,0:T(1,128)S(1)} %all-to-all-done.got, f32[17,8,128]{2,1,0:T(8,128)S(1)} %get-tuple-element.30.state.state_in, f32[6,8,128]{2,1,0:T(8,128)S(1)} %get-tuple-element.33.sums, s32[8,32]{1,0:T(8,128)S(4)} %get-tuple-element.34.plan.rest_1_), custom_call_target="tpu_custom_call" | custom-call | tf_op jit(solution)/shard_map/after1/pallas_call | solution.py:594
  76.1 9.7 %all-to-all-start.2 = ((f32[256,1,384]{2,1,0:T(1,128)}), f32[256,1,384]{2,1,0:T(1,128)S(1)}, u32[]{:S(2)}, u32[]{:S(2)}) async-start(f32[256,1,384]{2,1,0:T(1,128)} %get-tuple-element.35), calls=%async_computation.2 | async-start | bytes 786432 | tf_op jit(solution)/shard_map/all_to_all | solution.py:532
  85.8 0.0 copy-done.1
  85.8 10.1 %ahead2.1 = (f32[4,8,128]{2,1,0:T(8,128)S(1)}, s32[8,32]{1,0:T(8,128)S(4)}, f32[3,8,128]{2,1,0:T(8,128)S(1)}, f32[2,8,128]{2,1,0:T(8,128)S(1)}) custom-call(s32[1]{0:T(128)} %bitcast.me, f32[16,120,128]{2,1,0:T(8,128)S(1)} %bitcast.10, f32[16,96,128]{2,1,0:T(8,128)S(1)} %copy-done.1, s32[16]{0:T(128)} %lev.9, s32[16,16]{1,0:T(8,128)} %convert_bitcast_fusion.levall, ...), custom_call_target="tpu_custom_call" | custom-call | tf_op jit(solution)/shard_map/ahead2/pallas_call | solution.py:571
  95.8 0.0 copy-start.2
  95.9 8.2 %all-to-all-done.2.got = f32[256,1,384]{2,1,0:T(1,128)S(1)} async-done(((f32[256,1,384]{2,1,0:T(1,128)}), f32[256,1,384]{2,1,0:T(1,128)S(1)}, u32[]{:S(2)}, u32[]{:S(2)}) %all-to-all-start.2) | async-done | bytes 393248 | tf_op jit(solution)/shard_map/all_to_all | solution.py:532
  104.1 5.3 %after2.1 = (f32[17,8,128]{2,1,0:T(8,128)S(1)}, f32[256,1,384]{2,1,0:T(1,128)}) custom-call(f32[256,1,384]{2,1,0:T(1,128)S(1)} %all-to-all-done.2.got, f32[17,8,128]{2,1,0:T(8,128)S(1)} %get-tuple-element.36.state.state_in, f32[4,8,128]{2,1,0:T(8,128)S(1)} %get-tuple-element.38.sums, s32[8,32]{1,0:T(8,128)S(4)} %get-tuple-element.39.plan, ...), custom_call_target="tpu_custom_call" | custom-call | tf_op jit(solution)/shard_map/after2/pallas_call | solution.py:594
  109.4 5.2 %all-to-all-start.3 = ((f32[256,1,384]{2,1,0:T(1,128)}), f32[256,1,384]{2,1,0:T(1,128)S(1)}, u32[]{:S(2)}, u32[]{:S(2)}) async-start(f32[256,1,384]{2,1,0:T(1,128)} %get-tuple-element.42), calls=%async_computation.3 | async-start | bytes 786432 | tf_op jit(solution)/shard_map/all_to_all | solution.py:532
  114.7 0.0 copy-done.2
  114.7 7.1 %ahead3.1 = (f32[8,8,128]{2,1,0:T(8,128)S(1)}, s32[8,32]{1,0:T(8,128)S(4)}) custom-call(s32[1]{0:T(128)} %bitcast.me, f32[16,120,128]{2,1,0:T(8,128)S(1)} %bitcast.11, f32[16,96,128]{2,1,0:T(8,128)S(1)} %copy-done.2, s32[16]{0:T(128)} %lev.9, s32[16,16]{1,0:T(8,128)} %convert_bitcast_fusion.levall, s32[16]{0:T(128)} %partner.7, ...), custom_call_target="tpu_custom_call" | custom-call | tf_op jit(solution)/shard_map/ahead3/pallas_call | solution.py:571
  121.7 11.3 %all-to-all-done.3.got = f32[256,1,384]{2,1,0:T(1,128)S(1)} async-done(((f32[256,1,384]{2,1,0:T(1,128)}), f32[256,1,384]{2,1,0:T(1,128)S(1)}, u32[]{:S(2)}, u32[]{:S(2)}) %all-to-all-start.3) | async-done | bytes 393248 | tf_op jit(solution)/shard_map/all_to_all | solution.py:532
  133.0 6.4 %after3.1 = f32[16,1,1152]{2,1,0:T(1,128)} custom-call(f32[256,1,384]{2,1,0:T(1,128)S(1)} %all-to-all-done.3.got, f32[17,8,128]{2,1,0:T(8,128)S(1)} %get-tuple-element.43.state.state_in, f32[8,8,128]{2,1,0:T(8,128)S(1)} %get-tuple-element.45.sums, s32[8,32]{1,0:T(8,128)S(4)} %get-tuple-element.46.plan, f32[8,8,256]{2,1,0:T(8,128)S(1)} %get-tuple-element.40.rest_0_, ...), custom_call_target="tpu_custom_call" | custom-call | tf_op jit(solution)/shard_map/after3/pallas_call | solution.py:594
  139.4 13.0 %all_to_all.25.got = f32[16,1,1152]{2,1,0:T(1,128)S(1)} all-to-all(f32[16,1,1152]{2,1,0:T(1,128)} %after3.1), channel_id=1, replica_groups=mesh['blk'=16,'grp'=16] {'grp'}, dimensions={0} | all-to-all | bytes 147456 | tf_op jit(solution)/shard_map/all_to_all | solution.py:532
  152.4 2.3 %last.1 = (f32[6,2048]{1,0:T(8,128)}, f32[6,2048]{1,0:T(8,128)}, f32[6,2048]{1,0:T(8,128)}) custom-call(f32[16,1,1152]{2,1,0:T(1,128)S(1)} %all_to_all.25.got, f32[6,2048]{1,0:T(8,128)} %ps.3, f32[6,2048]{1,0:T(8,128)} %fr.3, f32[6,2048]{1,0:T(8,128)} %irr.1, s32[8,32]{1,0:T(8,128)S(4)} %get-tuple-element.46.plan), custom_call_target="tpu_custom_call" | custom-call | tf_op jit(solution)/shard_map/last/pallas_call | solution.py:615
  (1 shorter events, 0.0 us)
Async XLA Ops:
  26.7 15.8 %all-to-all-start.1 = ((f32[16,96,128]{2,1,0:T(8,128)}), f32[16,96,128]{2,1,0:T(8,128)S(1)}, u32[]{:S(2)}, u32[]{:S(2)}) async-start(f32[16,96,128]{2,1,0:T(8,128)} %get-tuple-element.31), calls=%async_computation.1 | async-start | bytes 1572864 | tf_op jit(solution)/shard_map/all_to_all | solution.py:532
  42.5 20.7 %copy-start = (f32[16,96,128]{2,1,0:T(8,128)}, f32[16,96,128]{2,1,0:T(8,128)S(1)}, u32[]{:S(2)}) copy-start(f32[16,96,128]{2,1,0:T(8,128)S(1)} %all-to-all-done.1.rates) | copy-start | bytes 2359300
  42.5 29.0 %all-to-all-start = ((f32[256,1,256]{2,1,0:T(1,128)}), f32[256,1,256]{2,1,0:T(1,128)S(1)}, u32[]{:S(2)}, u32[]{:S(2)}) async-start(f32[256,1,256]{2,1,0:T(1,128)} %get-tuple-element.29), calls=%async_computation | async-start | bytes 524288 | tf_op jit(solution)/shard_map/all_to_all | solution.py:532
  71.5 14.3 %copy-start.1 = (f32[16,96,128]{2,1,0:T(8,128)S(1)}, f32[16,96,128]{2,1,0:T(8,128)}, u32[]{:S(2)}) copy-start(f32[16,96,128]{2,1,0:T(8,128)} %copy-done) | copy-start | bytes 2359300
  76.1 28.0 %all-to-all-start.2 = ((f32[256,1,384]{2,1,0:T(1,128)}), f32[256,1,384]{2,1,0:T(1,128)S(1)}, u32[]{:S(2)}, u32[]{:S(2)}) async-start(f32[256,1,384]{2,1,0:T(1,128)} %get-tuple-element.35), calls=%async_computation.2 | async-start | bytes 786432 | tf_op jit(solution)/shard_map/all_to_all | solution.py:532
  95.8 18.8 %copy-start.2 = (f32[16,96,128]{2,1,0:T(8,128)S(1)}, f32[16,96,128]{2,1,0:T(8,128)}, u32[]{:S(2)}) copy-start(f32[16,96,128]{2,1,0:T(8,128)} %copy-done) | copy-start | bytes 2359300
  109.4 23.6 %all-to-all-start.3 = ((f32[256,1,384]{2,1,0:T(1,128)}), f32[256,1,384]{2,1,0:T(1,128)S(1)}, u32[]{:S(2)}, u32[]{:S(2)}) async-start(f32[256,1,384]{2,1,0:T(1,128)} %get-tuple-element.42), calls=%async_computation.3 | async-start | bytes 786432 | tf_op jit(solution)/shard_map/all_to_all | solution.py:532

commit v2 on v1

--- a/solution.py
+++ b/solution.py
@@ -10,6 +10,7 @@
 CLOSE = 0.0001
 TICK = 0.125
 NB = 16
+SHIFT = 4
 BS = 128
 W = NB * BS
 F32 = jnp.float32
@@ -59,6 +60,7 @@
 
 
 BLOCK, PLACE, LEVEL, SHARD, ROW, HERE, COUNT = range(7)
+OWN, MATE, RANK, MATELEVEL, ME = range(5)
 
 
 def fill_slots(lev, top, cap, plan):
@@ -70,7 +72,7 @@
     for group in ((2,), (0, 1)) if top == 2 else ((0, 1),):
         ones = [jnp.int32(0), jnp.int32(4)]
         for k in range(NB):
-            level = lev[k]
+            level = lev(k)
             place = jnp.where(level == 0, ones[0], jnp.where(level == 1, ones[1], -1000))
             live = (level == 2) if group == (2,) else level <= min(top, 1)
             plan[BLOCK, count] = k
@@ -84,17 +86,15 @@
     plan[COUNT, 0] = count
 
 
-def fill_near(plan, cap, own, levall, partner, sent):
+def fill_near(plan, cap, known, sent):
+    me = known[ME, 0]
+
     def slot(s, _):
         k = plan[BLOCK, s]
-        q = partner[k] // NB
-        level = levall[q, k]
-        place = jnp.where(level == 0, 0, 4)
-        for e in range(NB):
-            place = place + ((levall[q, e] == level) & (e < k)).astype(jnp.int32)
+        q = known[MATE, k]
         ours = plan[LEVEL, s] <= sent
-        theirs = (q != own) & (level <= sent)
-        for e, (b, row, here) in enumerate(((own, plan[PLACE, s], ours), (q, place, theirs))):
+        theirs = (q != me) & (known[MATELEVEL, k] <= sent)
+        for e, (b, row, here) in enumerate(((me, plan[PLACE, s], ours), (q, known[RANK, k], theirs))):
             plan[SHARD, 2 * s + e] = b
             plan[ROW, 2 * s + e] = jnp.clip(jnp.where(here, row, 0), 0, 3 if sent == 0 else 7)
             plan[HERE, 2 * s + e] = here.astype(jnp.int32)
@@ -305,7 +305,7 @@
     parts = []
     seen = jnp.int32(4)
     for k in range(NB):
-        one = lev[k] == 1
+        one = lev(k) == 1
         mark = jnp.where(one, seen, -1000)
         x, v, a, j = columns(state[k])
         for f, column in enumerate(forecast(x, v, a, j, 2 * TICK)):
@@ -343,10 +343,14 @@
         rates[b] = rates[0]
 
 
-def first_kernel(me, col, table, mine, lev, levall, partner, state, pay, order0, order1, turned, plan):
+def first_kernel(me, col, table, mine, lev, levall, partner, state, pay, order0, order1, known, turned, plan):
     me = me[0]
     col = pl.multiple_of(col[0] * 8, 8)
-    fill_slots(lev, TOP[0], CAPS[0], plan)
+    known[ME, 0] = me
+    for k in range(NB):
+        known[OWN, k] = lev[k]
+        known[MATE, k] = partner[k] >> SHIFT
+    fill_slots(lambda k: lev[k], TOP[0], CAPS[0], plan)
     for k in range(NB):
         turned[k, :, 0:16] = mine[k].T
     for k in range(NB):
@@ -360,7 +364,7 @@
 
     def close(s, e, part):
         k = plan[BLOCK, s]
-        b = partner[k] // NB if part else me
+        b = known[MATE, k] if part else me
         rows, mass = from_table(table, b, k)
         return rows, mass, b != me if part else jnp.bool_(True)
 
@@ -370,12 +374,18 @@
     def sweep(goal):
         def group(b, carry):
             acc, counts = carry
+            ranks = [jnp.int32(0), jnp.int32(4)]
             for k in range(NB):
                 rows, mass = from_table(table, b, k)
                 acc = tuple(pair(goal[e], rows, mass, WIDE, acc[e]) for e in range(2))
                 for order, count in zip(orders, counts):
                     order[count] = b * NB + k
-                counts = tuple(counts[e] + (levall[b, k] > e).astype(jnp.int32) for e in range(2))
+                level = levall[b, k]
+                counts = tuple(counts[e] + (level > e).astype(jnp.int32) for e in range(2))
+                at = jnp.where(known[MATE, k] == b, k, 31)
+                known[RANK, at] = jnp.where(level == 0, ranks[0], ranks[1])
+                known[MATELEVEL, at] = level
+                ranks = [ranks[e] + (level == e).astype(jnp.int32) for e in range(2)]
             return acc, counts
 
         start = ((zeros(), zeros()), (jnp.int32(0), jnp.int32(0)))
@@ -399,7 +409,7 @@
 
     def load(g, e):
         index = order[g * NB + e]
-        return from_predicted(predicted, index // NB, lax.rem(index, NB))
+        return from_predicted(predicted, index >> SHIFT, index & (NB - 1))
 
     def close(s, e, part):
         rows, mass = from_predicted(predicted, plan[SHARD, 2 * s + part], plan[BLOCK, s])
@@ -422,16 +432,17 @@
     return jnp.minimum(plan[COUNT, 2] // 2, 1)
 
 
-def ahead_kernel(step, me, table, rates, lev, levall, partner, order, state, *rest):
+def ahead_kernel(step, known, table, rates, order, state, *rest):
     if step == 1:
         sums, plan, predicted = rest
     elif step == 2:
         sums, plan, later, early, predicted, plan3 = rest
     else:
         early, sums, plan, predicted = rest
-    me = me[0]
+    me = known[ME, 0]
+    lev = lambda k: known[OWN, k]
     fill_slots(lev, TOP[step], CAPS[step], plan)
-    fill_near(plan, CAPS[step], me, levall, partner, SENT[step])
+    fill_near(plan, CAPS[step], known, SENT[step])
     fill_sources(table, rates, predicted, step * TICK)
     first = 0
     if step == 3:
@@ -441,7 +452,7 @@
     if step == 2:
         fill_later(state, lev, later)
         fill_slots(lev, TOP[3], CAPS[3], plan3)
-        fill_near(plan3, 2, me, levall, partner, SENT[3])
+        fill_near(plan3, 2, known, SENT[3])
         fill_sources(table, rates, predicted, 3 * TICK)
         early[...] = jnp.zeros((2, 8, 128), F32)
         ahead_sums(3, 0, early_pairs(plan3), me, plan3, order, predicted, state, early)
@@ -533,7 +544,7 @@
 
     packed, rates, mine = pl.pallas_call(
         pack_kernel,
-        out_shape=(array(7 * NB + 8, BS), array(shards, 6 * NB, BS), near(NB, 16, BS)),
+        out_shape=(near(7 * NB + 8, BS), array(shards, 6 * NB, BS), near(NB, 16, BS)),
         in_specs=[VMEM, VMEM, VMEM, SMEM],
         out_specs=(VMEM, VMEM, VMEM),
         name="pack",
@@ -543,11 +554,12 @@
     table, rates = lax.optimization_barrier((table, rates))
     rates = exchange(rates, "blk")
     order_shape = pltpu.SMEM(((shards + 3) * NB,), jnp.int32)
-    state, pay, *orders = pl.pallas_call(
+    known_shape = pltpu.SMEM((8, 32), jnp.int32)
+    state, pay, *orders, known = pl.pallas_call(
         first_kernel,
-        out_shape=(state_shape, array(everyone, 1, 256), order_shape, order_shape),
+        out_shape=(state_shape, array(everyone, 1, 256), order_shape, order_shape, known_shape),
         in_specs=[SMEM, SMEM, VMEM, VMEM, SMEM, SMEM, SMEM],
-        out_specs=(VMEM, VMEM, SMEM, SMEM),
+        out_specs=(VMEM, VMEM, SMEM, SMEM, SMEM),
         scratch_shapes=[pltpu.VMEM((NB, 128, 128), F32), pltpu.SMEM((8, 32), jnp.int32)],
         name="first",
     )(me, col, here(table), here(mine), levels, levall, partner)
@@ -556,8 +568,8 @@
         cap = CAPS[step]
         lanes = (0, 256, 384, 384)[step]
         got = exchange(pay, ("blk", "grp"))
-        ins = (me, here(table), here(rates), levels, levall, partner, kept(orders[SENT[step]]), here(state))
-        specs = [SMEM, VMEM, VMEM, SMEM, SMEM, SMEM, SMEM, VMEM]
+        ins = (kept(known), here(table), here(rates), kept(orders[SENT[step]]), here(state))
+        specs = [SMEM, VMEM, VMEM, SMEM, VMEM]
         out_shape = (near(cap, 8, 128), plan_shape)
         out_specs = (VMEM, SMEM)
         scratch = [pltpu.VMEM((shards + 1, QUANTITIES, NB, BS), F32)]

time: 158 us -> 156 us (0.987)
  Pallas kernels: 54.6 us -> 43.7 us
  waiting for transfers between devices: 29.6 us -> 38.4 us
    all_to_all x4, waiting for transfers between devices: 29.6 us -> 38.4 us  [exchange(): return lax.all_to_all(pay, axis, split_axis=0, concat_axis=0, tiled=True)]
    pallas_call x3, Pallas kernels: 24.4 us -> 19.4 us  [body(): pl.pallas_call(functools.partial(ahead_kernel, step), out_shape=out_shape...]
    pallas_call x1, Pallas kernels: 9.73 us -> 6 us  [body(): pl.pallas_call(first_kernel, out_shape=(state_shape, array(everyone, 1, 2...]
    pallas_call x3, Pallas kernels: 16.3 us -> 14.2 us  [body(): pl.pallas_call(functools.partial(after_kernel, step), out_shape=out_shape...]
  transfers between devices with their start and end apart: 4 -> 4, of which waited for: 4 -> 4; matrix products, arithmetic and copies ran while one was open for 0% -> 0% of each run, Pallas kernels for 22% -> 16%
where the time goes in v2:
time: 156 us; the launch traced here: 154 us
  Pallas kernels  43.7 us (28%)
  waiting for transfers between devices  38.4 us (25%)
  blocking collectives  37.3 us (24%)
  starting transfers between devices  33.2 us (21%)
    all_to_all x4, waiting for transfers between devices, exchange(): return lax.all_to_all(pay, axis, split_axis=0, concat_axis=0, tiled=True)  38.4 us
    all_to_all x4, starting transfers between devices, exchange(): return lax.all_to_all(pay, axis, split_axis=0, concat_axis=0, tiled=True)  33.2 us
    all_gather x1, blocking collectives, body(): table = lax.all_gather(packed, 'blk', axis=0, tiled=False)  23.9 us
    pallas_call x3, Pallas kernels, body(): pl.pallas_call(functools.partial(ahead_kernel, step), out_shape=out_shape...  19.4 us
    pallas_call x3, Pallas kernels, body(): pl.pallas_call(functools.partial(after_kernel, step), out_shape=out_shape...  14.2 us
    all_to_all x1, blocking collectives, exchange(): return lax.all_to_all(pay, axis, split_axis=0, concat_axis=0, tiled=True)  13.4 us
    pallas_call x1, Pallas kernels, body(): pl.pallas_call(first_kernel, out_shape=(state_shape, array(everyone, 1, 2...  6 us
  transfers between devices with their start and end apart: 4, of which 4 were waited for; matrix products, arithmetic and copies ran while one was open for 0% of the time, Pallas kernels for 16%

profile of v2, /device:TPU:1, one launch (start us, length us, event | category | flops | bytes accessed | tf_op | source)
XLA Modules:
  0.0 154.0 jit_solution(9420883972980749800)
XLA Ops:
  0.6 1.9 %pack.1 = (f32[120,128]{1,0:T(8,128)S(1)}, f32[16,96,128]{2,1,0:T(8,128)}, f32[16,16,128]{2,1,0:T(8,128)S(1)}) custom-call(f32[6,2048]{1,0:T(8,128)} %ps.3, f32[6,2048]{1,0:T(8,128)} %fr.3, f32[1,2048]{1,0:T(1,128)} %bitcast.11, s32[16]{0:T(128)} %lev.3), custom_call_target="tpu_custom_call" | custom-call | tf_op jit(solution)/shard_map/pack/pallas_call | solution.py:545
  2.6 23.9 %all-gather = f32[1920,128]{1,0:T(8,128)S(1)} all-gather(f32[120,128]{1,0:T(8,128)S(1)} %get-tuple-element.26), channel_id=2, replica_groups=mesh['blk'=16,'grp'=16] {'blk'}, dimensions={0}, use_global_device_ids=true | all-gather | bytes 1044480 | tf_op jit(solution)/shard_map/all_gather | solution.py:552
  26.5 3.6 %all-to-all-start.1 = ((f32[16,96,128]{2,1,0:T(8,128)}), f32[16,96,128]{2,1,0:T(8,128)S(1)}, u32[]{:S(2)}, u32[]{:S(2)}) async-start(f32[16,96,128]{2,1,0:T(8,128)} %get-tuple-element.33), calls=%async_computation.1 | async-start | bytes 1572864 | tf_op jit(solution)/shard_map/all_to_all | solution.py:543
  30.1 0.6 slice_convert_fusion
  30.7 6.0 %first.1 = (f32[17,8,128]{2,1,0:T(8,128)S(1)}, f32[256,1,256]{2,1,0:T(1,128)}, s32[304]{0:T(512)S(4)}, s32[304]{0:T(512)S(4)}, s32[8,32]{1,0:T(8,128)S(4)}) custom-call(s32[1]{0:T(128)} %bitcast.me, s32[1]{0:T(128)} %bitcast.1.col, f32[16,120,128]{2,1,0:T(8,128)S(1)} %bitcast.6, f32[16,16,128]{2,1,0:T(8,128)S(1)} %get-tuple-element.29.mine, s32[16]{0:T(128)} %lev.3, ...), custom_call_target="tpu_custom_call" | custom-call | tf_op jit(solution)/shard_map/first/pallas_call | solution.py:558
  36.7 5.6 %all-to-all-done.1.rates = f32[16,96,128]{2,1,0:T(8,128)S(1)} async-done(((f32[16,96,128]{2,1,0:T(8,128)}), f32[16,96,128]{2,1,0:T(8,128)S(1)}, u32[]{:S(2)}, u32[]{:S(2)}) %all-to-all-start.1) | async-done | bytes 786464 | tf_op jit(solution)/shard_map/all_to_all | solution.py:543
  42.3 0.0 copy-start
  42.3 13.4 %all-to-all-start = ((f32[256,1,256]{2,1,0:T(1,128)}), f32[256,1,256]{2,1,0:T(1,128)S(1)}, u32[]{:S(2)}, u32[]{:S(2)}) async-start(f32[256,1,256]{2,1,0:T(1,128)} %get-tuple-element.30), calls=%async_computation | async-start | bytes 524288 | tf_op jit(solution)/shard_map/all_to_all | solution.py:543
  55.7 6.5 %ahead1.1 = (f32[6,8,128]{2,1,0:T(8,128)S(1)}, s32[8,32]{1,0:T(8,128)S(4)}) custom-call(s32[8,32]{1,0:T(8,128)S(4)} %get-tuple-element.32.known, f32[16,120,128]{2,1,0:T(8,128)S(1)} %bitcast.7, f32[16,96,128]{2,1,0:T(8,128)S(1)} %all-to-all-done.1.rates, s32[304]{0:T(512)S(4)} %get-tuple-element.34.order, f32[17,8,128]{2,1,0:T(8,128)S(1)} %get-tuple-element.31.state.state_in), custom_call_target="tpu_custom_call" | custom-call | tf_op jit(solution)/shard_map/ahead1/pallas_call | solution.py:583
  62.2 0.0 copy-done
  62.2 9.1 %all-to-all-done.got = f32[256,1,256]{2,1,0:T(1,128)S(1)} async-done(((f32[256,1,256]{2,1,0:T(1,128)}), f32[256,1,256]{2,1,0:T(1,128)S(1)}, u32[]{:S(2)}, u32[]{:S(2)}) %all-to-all-start) | async-done | bytes 262176 | tf_op jit(solution)/shard_map/all_to_all | solution.py:543
  71.2 0.0 copy-start.1
  71.3 4.6 %after1.1 = (f32[17,8,128]{2,1,0:T(8,128)S(1)}, f32[256,1,384]{2,1,0:T(1,128)}, f32[8,8,256]{2,1,0:T(8,128)S(1)}) custom-call(f32[256,1,256]{2,1,0:T(1,128)S(1)} %all-to-all-done.got, f32[17,8,128]{2,1,0:T(8,128)S(1)} %get-tuple-element.31.state.state_in, f32[6,8,128]{2,1,0:T(8,128)S(1)} %get-tuple-element.35.sums, s32[8,32]{1,0:T(8,128)S(4)} %get-tuple-element.36.plan.rest_1_), custom_call_target="tpu_custom_call" | custom-call | tf_op jit(solution)/shard_map/after1/pallas_call | solution.py:606
  75.8 9.3 %all-to-all-start.2 = ((f32[256,1,384]{2,1,0:T(1,128)}), f32[256,1,384]{2,1,0:T(1,128)S(1)}, u32[]{:S(2)}, u32[]{:S(2)}) async-start(f32[256,1,384]{2,1,0:T(1,128)} %get-tuple-element.37), calls=%async_computation.2 | async-start | bytes 786432 | tf_op jit(solution)/shard_map/all_to_all | solution.py:543
  85.1 0.0 copy-done.1
  85.1 4.0 %ahead2.1 = (f32[4,8,128]{2,1,0:T(8,128)S(1)}, s32[8,32]{1,0:T(8,128)S(4)}, f32[3,8,128]{2,1,0:T(8,128)S(1)}, f32[2,8,128]{2,1,0:T(8,128)S(1)}) custom-call(s32[8,32]{1,0:T(8,128)S(4)} %get-tuple-element.32.known, f32[16,120,128]{2,1,0:T(8,128)S(1)} %bitcast.8, f32[16,96,128]{2,1,0:T(8,128)S(1)} %copy-done.1, s32[304]{0:T(512)S(4)} %get-tuple-element.39.order, ...), custom_call_target="tpu_custom_call" | custom-call | tf_op jit(solution)/shard_map/ahead2/pallas_call | solution.py:583
  89.1 0.0 copy-start.2
  89.1 14.4 %all-to-all-done.2.got = f32[256,1,384]{2,1,0:T(1,128)S(1)} async-done(((f32[256,1,384]{2,1,0:T(1,128)}), f32[256,1,384]{2,1,0:T(1,128)S(1)}, u32[]{:S(2)}, u32[]{:S(2)}) %all-to-all-start.2) | async-done | bytes 393248 | tf_op jit(solution)/shard_map/all_to_all | solution.py:543
  103.4 3.3 %after2.1 = (f32[17,8,128]{2,1,0:T(8,128)S(1)}, f32[256,1,384]{2,1,0:T(1,128)}) custom-call(f32[256,1,384]{2,1,0:T(1,128)S(1)} %all-to-all-done.2.got, f32[17,8,128]{2,1,0:T(8,128)S(1)} %get-tuple-element.38.state.state_in, f32[4,8,128]{2,1,0:T(8,128)S(1)} %get-tuple-element.40.sums, s32[8,32]{1,0:T(8,128)S(4)} %get-tuple-element.41.plan, ...), custom_call_target="tpu_custom_call" | custom-call | tf_op jit(solution)/shard_map/after2/pallas_call | solution.py:606
  106.7 7.0 %all-to-all-start.3 = ((f32[256,1,384]{2,1,0:T(1,128)}), f32[256,1,384]{2,1,0:T(1,128)S(1)}, u32[]{:S(2)}, u32[]{:S(2)}) async-start(f32[256,1,384]{2,1,0:T(1,128)} %get-tuple-element.44), calls=%async_computation.3 | async-start | bytes 786432 | tf_op jit(solution)/shard_map/all_to_all | solution.py:543
  113.7 0.0 copy-done.2
  113.7 8.9 %ahead3.1 = (f32[8,8,128]{2,1,0:T(8,128)S(1)}, s32[8,32]{1,0:T(8,128)S(4)}) custom-call(s32[8,32]{1,0:T(8,128)S(4)} %get-tuple-element.32.known, f32[16,120,128]{2,1,0:T(8,128)S(1)} %bitcast.9, f32[16,96,128]{2,1,0:T(8,128)S(1)} %copy-done.2, s32[304]{0:T(512)S(4)} %get-tuple-element.39.order, f32[17,8,128]{2,1,0:T(8,128)S(1)} %get-tuple-element.45.state.state_in, ...), custom_call_target="tpu_custom_call" | custom-call | tf_op jit(solution)/shard_map/ahead3/pallas_call | solution.py:583
  122.7 9.4 %all-to-all-done.3.got = f32[256,1,384]{2,1,0:T(1,128)S(1)} async-done(((f32[256,1,384]{2,1,0:T(1,128)}), f32[256,1,384]{2,1,0:T(1,128)S(1)}, u32[]{:S(2)}, u32[]{:S(2)}) %all-to-all-start.3) | async-done | bytes 393248 | tf_op jit(solution)/shard_map/all_to_all | solution.py:543
  132.1 6.4 %after3.1 = f32[16,1,1152]{2,1,0:T(1,128)} custom-call(f32[256,1,384]{2,1,0:T(1,128)S(1)} %all-to-all-done.3.got, f32[17,8,128]{2,1,0:T(8,128)S(1)} %get-tuple-element.45.state.state_in, f32[8,8,128]{2,1,0:T(8,128)S(1)} %get-tuple-element.47.sums, s32[8,32]{1,0:T(8,128)S(4)} %get-tuple-element.48.plan, f32[8,8,256]{2,1,0:T(8,128)S(1)} %get-tuple-element.42.rest_0_, ...), custom_call_target="tpu_custom_call" | custom-call | tf_op jit(solution)/shard_map/after3/pallas_call | solution.py:606
  138.4 13.4 %all_to_all.25.got = f32[16,1,1152]{2,1,0:T(1,128)S(1)} all-to-all(f32[16,1,1152]{2,1,0:T(1,128)} %after3.1), channel_id=1, replica_groups=mesh['blk'=16,'grp'=16] {'grp'}, dimensions={0} | all-to-all | bytes 147456 | tf_op jit(solution)/shard_map/all_to_all | solution.py:543
  151.8 2.2 %last.1 = (f32[6,2048]{1,0:T(8,128)}, f32[6,2048]{1,0:T(8,128)}, f32[6,2048]{1,0:T(8,128)}) custom-call(f32[16,1,1152]{2,1,0:T(1,128)S(1)} %all_to_all.25.got, f32[6,2048]{1,0:T(8,128)} %ps.3, f32[6,2048]{1,0:T(8,128)} %fr.3, f32[6,2048]{1,0:T(8,128)} %irr.1, s32[8,32]{1,0:T(8,128)S(4)} %get-tuple-element.48.plan), custom_call_target="tpu_custom_call" | custom-call | tf_op jit(solution)/shard_map/last/pallas_call | solution.py:627
Async XLA Ops:
  26.5 15.8 %all-to-all-start.1 = ((f32[16,96,128]{2,1,0:T(8,128)}), f32[16,96,128]{2,1,0:T(8,128)S(1)}, u32[]{:S(2)}, u32[]{:S(2)}) async-start(f32[16,96,128]{2,1,0:T(8,128)} %get-tuple-element.33), calls=%async_computation.1 | async-start | bytes 1572864 | tf_op jit(solution)/shard_map/all_to_all | solution.py:543
  42.3 19.9 %copy-start = (f32[16,96,128]{2,1,0:T(8,128)}, f32[16,96,128]{2,1,0:T(8,128)S(1)}, u32[]{:S(2)}) copy-start(f32[16,96,128]{2,1,0:T(8,128)S(1)} %all-to-all-done.1.rates) | copy-start | bytes 2359300
  42.3 29.0 %all-to-all-start = ((f32[256,1,256]{2,1,0:T(1,128)}), f32[256,1,256]{2,1,0:T(1,128)S(1)}, u32[]{:S(2)}, u32[]{:S(2)}) async-start(f32[256,1,256]{2,1,0:T(1,128)} %get-tuple-element.30), calls=%async_computation | async-start | bytes 524288 | tf_op jit(solution)/shard_map/all_to_all | solution.py:543
  71.2 13.8 %copy-start.1 = (f32[16,96,128]{2,1,0:T(8,128)S(1)}, f32[16,96,128]{2,1,0:T(8,128)}, u32[]{:S(2)}) copy-start(f32[16,96,128]{2,1,0:T(8,128)} %copy-done) | copy-start | bytes 2359300
  75.8 27.6 %all-to-all-start.2 = ((f32[256,1,384]{2,1,0:T(1,128)}), f32[256,1,384]{2,1,0:T(1,128)S(1)}, u32[]{:S(2)}, u32[]{:S(2)}) async-start(f32[256,1,384]{2,1,0:T(1,128)} %get-tuple-element.37), calls=%async_computation.2 | async-start | bytes 786432 | tf_op jit(solution)/shard_map/all_to_all | solution.py:543
  89.1 24.7 %copy-start.2 = (f32[16,96,128]{2,1,0:T(8,128)S(1)}, f32[16,96,128]{2,1,0:T(8,128)}, u32[]{:S(2)}) copy-start(f32[16,96,128]{2,1,0:T(8,128)} %copy-done) | copy-start | bytes 2359300
  106.7 25.3 %all-to-all-start.3 = ((f32[256,1,384]{2,1,0:T(1,128)}), f32[256,1,384]{2,1,0:T(1,128)S(1)}, u32[]{:S(2)}, u32[]{:S(2)}) async-start(f32[256,1,384]{2,1,0:T(1,128)} %get-tuple-element.44), calls=%async_computation.3 | async-start | bytes 786432 | tf_op jit(solution)/shard_map/all_to_all | solution.py:543

commit v3 on v2

--- a/solution.py
+++ b/solution.py
@@ -599,7 +599,7 @@
         if step == 2:
             ins += (here(outs[2]),)
             specs += [VMEM]
-        pay_shape = array(everyone if step < 3 else columns_, 1, (0, 384, 384, 1152)[step])
+        pay_shape = array(everyone, 1, 384) if step < 3 else near(columns_, 1, 1152)
         out_shape = {
             1: (state_shape, pay_shape, near(8, 8, everyone)), 2: (state_shape, pay_shape), 3: (pay_shape,),
         }[step]
@@ -630,7 +630,7 @@
             in_specs=[VMEM, VMEM, VMEM, VMEM, SMEM],
             out_specs=(VMEM, VMEM, VMEM),
             name="last",
-        )(here(got), phase_space, force_rates, irregular, kept(plan))
+        )(here(got), here(phase_space), here(force_rates), here(irregular), kept(plan))
     )
 
 

time: 156 us -> 153 us (0.981)
  Pallas kernels: 43.7 us -> 37.5 us
  waiting for transfers between devices: 38.4 us -> 41.3 us
    all_to_all x4, waiting for transfers between devices: 38.4 us -> 41.3 us  [exchange(): return lax.all_to_all(pay, axis, split_axis=0, concat_axis=0, tiled=True)]
    pallas_call x3, Pallas kernels: 19.4 us -> 16.6 us  [body(): pl.pallas_call(functools.partial(ahead_kernel, step), out_shape=out_shape...]
    pallas_call x3, Pallas kernels: 14.2 us -> 11.8 us  [body(): pl.pallas_call(functools.partial(after_kernel, step), out_shape=out_shape...]
  transfers between devices with their start and end apart: 4 -> 4, of which waited for: 4 -> 4; matrix products, arithmetic and copies ran while one was open for 0% -> 0% of each run, Pallas kernels for 16% -> 15%
where the time goes in v3:
time: 153 us; the launch traced here: 150 us
  waiting for transfers between devices  41.3 us (27%)
  Pallas kernels  37.5 us (25%)
  blocking collectives  36.3 us (24%)
  starting transfers between devices  34 us (22%)
    all_to_all x4, waiting for transfers between devices, exchange(): return lax.all_to_all(pay, axis, split_axis=0, concat_axis=0, tiled=True)  41.3 us
    all_to_all x4, starting transfers between devices, exchange(): return lax.all_to_all(pay, axis, split_axis=0, concat_axis=0, tiled=True)  34 us
    all_gather x1, blocking collectives, body(): table = lax.all_gather(packed, 'blk', axis=0, tiled=False)  23.9 us
    pallas_call x3, Pallas kernels, body(): pl.pallas_call(functools.partial(ahead_kernel, step), out_shape=out_shape...  16.6 us
    all_to_all x1, blocking collectives, exchange(): return lax.all_to_all(pay, axis, split_axis=0, concat_axis=0, tiled=True)  12.4 us
    pallas_call x3, Pallas kernels, body(): pl.pallas_call(functools.partial(after_kernel, step), out_shape=out_shape...  11.8 us
    pallas_call x1, Pallas kernels, body(): pl.pallas_call(first_kernel, out_shape=(state_shape, array(everyone, 1, 2...  5.98 us
  transfers between devices with their start and end apart: 4, of which 4 were waited for; matrix products, arithmetic and copies ran while one was open for 0% of the time, Pallas kernels for 15%

profile of v3, /device:TPU:1, one launch (start us, length us, event | category | flops | bytes accessed | tf_op | source)
XLA Modules:
  0.0 150.4 jit_solution(1515359643777428964)
XLA Ops:
  0.6 1.9 %pack.1 = (f32[120,128]{1,0:T(8,128)S(1)}, f32[16,96,128]{2,1,0:T(8,128)}, f32[16,16,128]{2,1,0:T(8,128)S(1)}) custom-call(f32[6,2048]{1,0:T(8,128)} %ps.3, f32[6,2048]{1,0:T(8,128)} %fr.3, f32[1,2048]{1,0:T(1,128)} %bitcast.11, s32[16]{0:T(128)} %lev.3), custom_call_target="tpu_custom_call" | custom-call | tf_op jit(solution)/shard_map/pack/pallas_call | solution.py:545
  2.6 23.9 %all-gather = f32[1920,128]{1,0:T(8,128)S(1)} all-gather(f32[120,128]{1,0:T(8,128)S(1)} %get-tuple-element.26), channel_id=2, replica_groups=mesh['blk'=16,'grp'=16] {'blk'}, dimensions={0}, use_global_device_ids=true | all-gather | bytes 1044480 | tf_op jit(solution)/shard_map/all_gather | solution.py:552
  26.5 3.6 %all-to-all-start.1 = ((f32[16,96,128]{2,1,0:T(8,128)}), f32[16,96,128]{2,1,0:T(8,128)S(1)}, u32[]{:S(2)}, u32[]{:S(2)}) async-start(f32[16,96,128]{2,1,0:T(8,128)} %get-tuple-element.33), calls=%async_computation.1 | async-start | bytes 1572864 | tf_op jit(solution)/shard_map/all_to_all | solution.py:543
  30.0 0.6 slice_convert_fusion
  30.6 6.0 %first.1 = (f32[17,8,128]{2,1,0:T(8,128)S(1)}, f32[256,1,256]{2,1,0:T(1,128)}, s32[304]{0:T(512)S(4)}, s32[304]{0:T(512)S(4)}, s32[8,32]{1,0:T(8,128)S(4)}) custom-call(s32[1]{0:T(128)} %bitcast.me, s32[1]{0:T(128)} %bitcast.1.col, f32[16,120,128]{2,1,0:T(8,128)S(1)} %bitcast.6, f32[16,16,128]{2,1,0:T(8,128)S(1)} %get-tuple-element.29.mine, s32[16]{0:T(128)} %lev.3, ...), custom_call_target="tpu_custom_call" | custom-call | tf_op jit(solution)/shard_map/first/pallas_call | solution.py:558
  36.6 5.6 %all-to-all-done.1.rates = f32[16,96,128]{2,1,0:T(8,128)S(1)} async-done(((f32[16,96,128]{2,1,0:T(8,128)}), f32[16,96,128]{2,1,0:T(8,128)S(1)}, u32[]{:S(2)}, u32[]{:S(2)}) %all-to-all-start.1) | async-done | bytes 786464 | tf_op jit(solution)/shard_map/all_to_all | solution.py:543
  42.2 0.0 copy-start
  42.2 13.4 %all-to-all-start = ((f32[256,1,256]{2,1,0:T(1,128)}), f32[256,1,256]{2,1,0:T(1,128)S(1)}, u32[]{:S(2)}, u32[]{:S(2)}) async-start(f32[256,1,256]{2,1,0:T(1,128)} %get-tuple-element.30), calls=%async_computation | async-start | bytes 524288 | tf_op jit(solution)/shard_map/all_to_all | solution.py:543
  55.7 6.5 %ahead1.1 = (f32[6,8,128]{2,1,0:T(8,128)S(1)}, s32[8,32]{1,0:T(8,128)S(4)}) custom-call(s32[8,32]{1,0:T(8,128)S(4)} %get-tuple-element.32.known, f32[16,120,128]{2,1,0:T(8,128)S(1)} %bitcast.7, f32[16,96,128]{2,1,0:T(8,128)S(1)} %all-to-all-done.1.rates, s32[304]{0:T(512)S(4)} %get-tuple-element.34.order, f32[17,8,128]{2,1,0:T(8,128)S(1)} %get-tuple-element.31.state.state_in), custom_call_target="tpu_custom_call" | custom-call | tf_op jit(solution)/shard_map/ahead1/pallas_call | solution.py:583
  62.2 0.0 copy-done
  62.2 9.1 %all-to-all-done.got = f32[256,1,256]{2,1,0:T(1,128)S(1)} async-done(((f32[256,1,256]{2,1,0:T(1,128)}), f32[256,1,256]{2,1,0:T(1,128)S(1)}, u32[]{:S(2)}, u32[]{:S(2)}) %all-to-all-start) | async-done | bytes 262176 | tf_op jit(solution)/shard_map/all_to_all | solution.py:543
  71.2 0.0 copy-start.1
  71.2 4.6 %after1.1 = (f32[17,8,128]{2,1,0:T(8,128)S(1)}, f32[256,1,384]{2,1,0:T(1,128)}, f32[8,8,256]{2,1,0:T(8,128)S(1)}) custom-call(f32[256,1,256]{2,1,0:T(1,128)S(1)} %all-to-all-done.got, f32[17,8,128]{2,1,0:T(8,128)S(1)} %get-tuple-element.31.state.state_in, f32[6,8,128]{2,1,0:T(8,128)S(1)} %get-tuple-element.35.sums, s32[8,32]{1,0:T(8,128)S(4)} %get-tuple-element.36.plan.rest_1_), custom_call_target="tpu_custom_call" | custom-call | tf_op jit(solution)/shard_map/after1/pallas_call | solution.py:606
  75.8 9.0 %all-to-all-start.2 = ((f32[256,1,384]{2,1,0:T(1,128)}), f32[256,1,384]{2,1,0:T(1,128)S(1)}, u32[]{:S(2)}, u32[]{:S(2)}) async-start(f32[256,1,384]{2,1,0:T(1,128)} %get-tuple-element.37), calls=%async_computation.2 | async-start | bytes 786432 | tf_op jit(solution)/shard_map/all_to_all | solution.py:543
  84.9 0.0 copy-done.1
  84.9 4.0 %ahead2.1 = (f32[4,8,128]{2,1,0:T(8,128)S(1)}, s32[8,32]{1,0:T(8,128)S(4)}, f32[3,8,128]{2,1,0:T(8,128)S(1)}, f32[2,8,128]{2,1,0:T(8,128)S(1)}) custom-call(s32[8,32]{1,0:T(8,128)S(4)} %get-tuple-element.32.known, f32[16,120,128]{2,1,0:T(8,128)S(1)} %bitcast.8, f32[16,96,128]{2,1,0:T(8,128)S(1)} %copy-done.1, s32[304]{0:T(512)S(4)} %get-tuple-element.39.order, ...), custom_call_target="tpu_custom_call" | custom-call | tf_op jit(solution)/shard_map/ahead2/pallas_call | solution.py:583
  88.8 0.0 copy-start.2
  88.9 14.4 %all-to-all-done.2.got = f32[256,1,384]{2,1,0:T(1,128)S(1)} async-done(((f32[256,1,384]{2,1,0:T(1,128)}), f32[256,1,384]{2,1,0:T(1,128)S(1)}, u32[]{:S(2)}, u32[]{:S(2)}) %all-to-all-start.2) | async-done | bytes 393248 | tf_op jit(solution)/shard_map/all_to_all | solution.py:543
  103.2 3.3 %after2.1 = (f32[17,8,128]{2,1,0:T(8,128)S(1)}, f32[256,1,384]{2,1,0:T(1,128)}) custom-call(f32[256,1,384]{2,1,0:T(1,128)S(1)} %all-to-all-done.2.got, f32[17,8,128]{2,1,0:T(8,128)S(1)} %get-tuple-element.38.state.state_in, f32[4,8,128]{2,1,0:T(8,128)S(1)} %get-tuple-element.40.sums, s32[8,32]{1,0:T(8,128)S(4)} %get-tuple-element.41.plan, ...), custom_call_target="tpu_custom_call" | custom-call | tf_op jit(solution)/shard_map/after2/pallas_call | solution.py:606
  106.5 8.0 %all-to-all-start.3 = ((f32[256,1,384]{2,1,0:T(1,128)}), f32[256,1,384]{2,1,0:T(1,128)S(1)}, u32[]{:S(2)}, u32[]{:S(2)}) async-start(f32[256,1,384]{2,1,0:T(1,128)} %get-tuple-element.44), calls=%async_computation.3 | async-start | bytes 786432 | tf_op jit(solution)/shard_map/all_to_all | solution.py:543
  114.6 0.0 copy-done.2
  114.6 6.2 %ahead3.1 = (f32[8,8,128]{2,1,0:T(8,128)S(1)}, s32[8,32]{1,0:T(8,128)S(4)}) custom-call(s32[8,32]{1,0:T(8,128)S(4)} %get-tuple-element.32.known, f32[16,120,128]{2,1,0:T(8,128)S(1)} %bitcast.9, f32[16,96,128]{2,1,0:T(8,128)S(1)} %copy-done.2, s32[304]{0:T(512)S(4)} %get-tuple-element.39.order, f32[17,8,128]{2,1,0:T(8,128)S(1)} %get-tuple-element.45.state.state_in, ...), custom_call_target="tpu_custom_call" | custom-call | tf_op jit(solution)/shard_map/ahead3/pallas_call | solution.py:583
  120.8 12.3 %all-to-all-done.3.got = f32[256,1,384]{2,1,0:T(1,128)S(1)} async-done(((f32[256,1,384]{2,1,0:T(1,128)}), f32[256,1,384]{2,1,0:T(1,128)S(1)}, u32[]{:S(2)}, u32[]{:S(2)}) %all-to-all-start.3) | async-done | bytes 393248 | tf_op jit(solution)/shard_map/all_to_all | solution.py:543
  133.0 0.0 copy-start.5
  133.1 3.9 %after3.1 = f32[16,1,1152]{2,1,0:T(1,128)S(1)} custom-call(f32[256,1,384]{2,1,0:T(1,128)S(1)} %all-to-all-done.3.got, f32[17,8,128]{2,1,0:T(8,128)S(1)} %get-tuple-element.45.state.state_in, f32[8,8,128]{2,1,0:T(8,128)S(1)} %get-tuple-element.47.sums, s32[8,32]{1,0:T(8,128)S(4)} %get-tuple-element.48.plan, f32[8,8,256]{2,1,0:T(8,128)S(1)} %get-tuple-element.42.rest_0_, ...), custom_call_target="tpu_custom_call" | custom-call | tf_op jit(solution)/shard_map/after3/pallas_call | solution.py:606
  137.0 0.0 copy-start.3
  137.0 0.0 copy-start.4
  137.0 12.4 %all_to_all.25.got = f32[16,1,1152]{2,1,0:T(1,128)S(1)} all-to-all(f32[16,1,1152]{2,1,0:T(1,128)S(1)} %after3.1), channel_id=1, replica_groups=mesh['blk'=16,'grp'=16] {'grp'}, dimensions={0} | all-to-all | bytes 147456 | tf_op jit(solution)/shard_map/all_to_all | solution.py:543
  149.4 0.0 copy-done.5
  149.4 0.0 copy-done.3
  149.4 0.0 copy-done.4
  149.4 1.1 last.1
Async XLA Ops:
  26.5 15.8 %all-to-all-start.1 = ((f32[16,96,128]{2,1,0:T(8,128)}), f32[16,96,128]{2,1,0:T(8,128)S(1)}, u32[]{:S(2)}, u32[]{:S(2)}) async-start(f32[16,96,128]{2,1,0:T(8,128)} %get-tuple-element.33), calls=%async_computation.1 | async-start | bytes 1572864 | tf_op jit(solution)/shard_map/all_to_all | solution.py:543
  42.2 19.9 %copy-start = (f32[16,96,128]{2,1,0:T(8,128)}, f32[16,96,128]{2,1,0:T(8,128)S(1)}, u32[]{:S(2)}) copy-start(f32[16,96,128]{2,1,0:T(8,128)S(1)} %all-to-all-done.1.rates) | copy-start | bytes 2359300
  42.2 29.0 %all-to-all-start = ((f32[256,1,256]{2,1,0:T(1,128)}), f32[256,1,256]{2,1,0:T(1,128)S(1)}, u32[]{:S(2)}, u32[]{:S(2)}) async-start(f32[256,1,256]{2,1,0:T(1,128)} %get-tuple-element.30), calls=%async_computation | async-start | bytes 524288 | tf_op jit(solution)/shard_map/all_to_all | solution.py:543
  71.2 13.6 %copy-start.1 = (f32[16,96,128]{2,1,0:T(8,128)S(1)}, f32[16,96,128]{2,1,0:T(8,128)}, u32[]{:S(2)}) copy-start(f32[16,96,128]{2,1,0:T(8,128)} %copy-done) | copy-start | bytes 2359300
  75.8 27.4 %all-to-all-start.2 = ((f32[256,1,384]{2,1,0:T(1,128)}), f32[256,1,384]{2,1,0:T(1,128)S(1)}, u32[]{:S(2)}, u32[]{:S(2)}) async-start(f32[256,1,384]{2,1,0:T(1,128)} %get-tuple-element.37), calls=%async_computation.2 | async-start | bytes 786432 | tf_op jit(solution)/shard_map/all_to_all | solution.py:543
  88.8 25.7 %copy-start.2 = (f32[16,96,128]{2,1,0:T(8,128)S(1)}, f32[16,96,128]{2,1,0:T(8,128)}, u32[]{:S(2)}) copy-start(f32[16,96,128]{2,1,0:T(8,128)} %copy-done) | copy-start | bytes 2359300
  106.5 26.5 %all-to-all-start.3 = ((f32[256,1,384]{2,1,0:T(1,128)}), f32[256,1,384]{2,1,0:T(1,128)S(1)}, u32[]{:S(2)}, u32[]{:S(2)}) async-start(f32[256,1,384]{2,1,0:T(1,128)} %get-tuple-element.44), calls=%async_computation.3 | async-start | bytes 786432 | tf_op jit(solution)/shard_map/all_to_all | solution.py:543
  133.0 16.3 %copy-start.5 = (f32[6,2048]{1,0:T(8,128)S(1)}, f32[6,2048]{1,0:T(8,128)}, u32[]{:S(2)}) copy-start(f32[6,2048]{1,0:T(8,128)} %irr.1) | copy-start | bytes 147460
  137.0 12.4 %copy-start.3 = (f32[6,2048]{1,0:T(8,128)S(1)}, f32[6,2048]{1,0:T(8,128)}, u32[]{:S(2)}) copy-start(f32[6,2048]{1,0:T(8,128)} %ps.3) | copy-start | bytes 147460
  137.0 12.4 %copy-start.4 = (f32[6,2048]{1,0:T(8,128)S(1)}, f32[6,2048]{1,0:T(8,128)}, u32[]{:S(2)}) copy-start(f32[6,2048]{1,0:T(8,128)} %fr.3) | copy-start | bytes 147460

commit v4 on v3

--- a/solution.py
+++ b/solution.py
@@ -263,9 +263,20 @@
 
 
 def send(tiles, pay):
-    for t, tile in enumerate(tiles):
-        full = jnp.broadcast_to(tile[None], (pay.shape[0], 1, 128))
-        pay[:, :, pl.ds(t * 128, 128)] = full
+    if len(pay.shape) == 3 and pay.shape[1] == 1:
+        for t, tile in enumerate(tiles):
+            pay[:, :, pl.ds(t * 128, 128)] = jnp.broadcast_to(tile[None], (pay.shape[0], 1, 128))
+        return
+    count = len(tiles)
+    row = lax.broadcasted_iota(jnp.int32, (8, 128), 0)
+    wide = [jnp.broadcast_to(tile, (8, 128)) for tile in tiles]
+    for e in range(count):
+        part = lax.rem(row + 8 * e, count)
+        value = wide[0]
+        for t in range(1, count):
+            value = jnp.where(part == t, wide[t], value)
+        for m in range(e, pay.shape[0], count):
+            pay[m] = value
 
 
 def corrector(step, state, plan, sums):
@@ -557,7 +568,7 @@
     known_shape = pltpu.SMEM((8, 32), jnp.int32)
     state, pay, *orders, known = pl.pallas_call(
         first_kernel,
-        out_shape=(state_shape, array(everyone, 1, 256), order_shape, order_shape, known_shape),
+        out_shape=(state_shape, array(everyone * 2 // 8, 8, 128), order_shape, order_shape, known_shape),
         in_specs=[SMEM, SMEM, VMEM, VMEM, SMEM, SMEM, SMEM],
         out_specs=(VMEM, VMEM, SMEM, SMEM, SMEM),
         scratch_shapes=[pltpu.VMEM((NB, 128, 128), F32), pltpu.SMEM((8, 32), jnp.int32)],
@@ -567,7 +578,7 @@
     for step in (1, 2, 3):
         cap = CAPS[step]
         lanes = (0, 256, 384, 384)[step]
-        got = exchange(pay, ("blk", "grp"))
+        got = exchange(pay.reshape(everyone, 1, lanes), ("blk", "grp"))
         ins = (kept(known), here(table), here(rates), kept(orders[SENT[step]]), here(state))
         specs = [SMEM, VMEM, VMEM, SMEM, VMEM]
         out_shape = (near(cap, 8, 128), plan_shape)
@@ -599,7 +610,7 @@
         if step == 2:
             ins += (here(outs[2]),)
             specs += [VMEM]
-        pay_shape = array(everyone, 1, 384) if step < 3 else near(columns_, 1, 1152)
+        pay_shape = array(everyone * 3 // 8, 8, 128) if step < 3 else near(columns_, 1, 1152)
         out_shape = {
             1: (state_shape, pay_shape, near(8, 8, everyone)), 2: (state_shape, pay_shape), 3: (pay_shape,),
         }[step]

time: 153 us -> 154 us (level)
  Pallas kernels: 37.5 us -> 48.9 us
  waiting for transfers between devices: 41.3 us -> 33.6 us
  starting transfers between devices: 34 us -> 31.4 us
    all_to_all x4, waiting for transfers between devices: 41.3 us -> 33.6 us  [exchange(): return lax.all_to_all(pay, axis, split_axis=0, concat_axis=0, tiled=True)]
    pallas_call x3, Pallas kernels: 16.6 us -> 20.8 us  [body(): pl.pallas_call(functools.partial(ahead_kernel, step), out_shape=out_shape...]
    pallas_call x1, Pallas kernels: 5.98 us -> 9.55 us  [body(): pl.pallas_call(first_kernel, out_shape=(state_shape, array(everyone * 2 /...]
    pallas_call x3, Pallas kernels: 11.8 us -> 15.3 us  [body(): pl.pallas_call(functools.partial(after_kernel, step), out_shape=out_shape...]
    all_to_all x4, starting transfers between devices: 34 us -> 31.4 us  [exchange(): return lax.all_to_all(pay, axis, split_axis=0, concat_axis=0, tiled=True)]
  transfers between devices with their start and end apart: 4 -> 4, of which waited for: 4 -> 4; matrix products, arithmetic and copies ran while one was open for 0% -> 0% of each run, Pallas kernels for 15% -> 20%
where the time goes in v4:
time: 154 us; the launch traced here: 152 us
  Pallas kernels  48.9 us (32%)
  blocking collectives  36.3 us (24%)
  waiting for transfers between devices  33.6 us (22%)
  starting transfers between devices  31.4 us (20%)
    all_to_all x4, waiting for transfers between devices, exchange(): return lax.all_to_all(pay, axis, split_axis=0, concat_axis=0, tiled=True)  33.6 us
    all_to_all x4, starting transfers between devices, exchange(): return lax.all_to_all(pay, axis, split_axis=0, concat_axis=0, tiled=True)  31.4 us
    all_gather x1, blocking collectives, body(): table = lax.all_gather(packed, 'blk', axis=0, tiled=False)  23.9 us
    pallas_call x3, Pallas kernels, body(): pl.pallas_call(functools.partial(ahead_kernel, step), out_shape=out_shape...  20.8 us
    pallas_call x3, Pallas kernels, body(): pl.pallas_call(functools.partial(after_kernel, step), out_shape=out_shape...  15.3 us
    all_to_all x1, blocking collectives, exchange(): return lax.all_to_all(pay, axis, split_axis=0, concat_axis=0, tiled=True)  12.4 us
    pallas_call x1, Pallas kernels, body(): pl.pallas_call(first_kernel, out_shape=(state_shape, array(everyone * 2 /...  9.55 us
  transfers between devices with their start and end apart: 4, of which 4 were waited for; matrix products, arithmetic and copies ran while one was open for 0% of the time, Pallas kernels for 20%

profile of v4, /device:TPU:1, one launch (start us, length us, event | category | flops | bytes accessed | tf_op | source)
XLA Modules:
  0.0 151.5 jit_solution(11079336768045614354)
XLA Ops:
  0.6 1.9 %pack.1 = (f32[120,128]{1,0:T(8,128)S(1)}, f32[16,96,128]{2,1,0:T(8,128)}, f32[16,16,128]{2,1,0:T(8,128)S(1)}) custom-call(f32[6,2048]{1,0:T(8,128)} %ps.3, f32[6,2048]{1,0:T(8,128)} %fr.3, f32[1,2048]{1,0:T(1,128)} %bitcast.17, s32[16]{0:T(128)} %lev.3), custom_call_target="tpu_custom_call" | custom-call | tf_op jit(solution)/shard_map/pack/pallas_call | solution.py:556
  2.6 23.9 %all-gather = f32[1920,128]{1,0:T(8,128)S(1)} all-gather(f32[120,128]{1,0:T(8,128)S(1)} %get-tuple-element.26), channel_id=2, replica_groups=mesh['blk'=16,'grp'=16] {'blk'}, dimensions={0}, use_global_device_ids=true | all-gather | bytes 1044480 | tf_op jit(solution)/shard_map/all_gather | solution.py:563
  26.5 3.6 %all-to-all-start.1 = ((f32[16,96,128]{2,1,0:T(8,128)}), f32[16,96,128]{2,1,0:T(8,128)S(1)}, u32[]{:S(2)}, u32[]{:S(2)}) async-start(f32[16,96,128]{2,1,0:T(8,128)} %get-tuple-element.33), calls=%async_computation.1 | async-start | bytes 1572864 | tf_op jit(solution)/shard_map/all_to_all | solution.py:554
  30.0 0.6 slice_convert_fusion
  30.6 9.5 %first.1 = (f32[17,8,128]{2,1,0:T(8,128)S(1)}, f32[64,8,128]{2,1,0:T(8,128)}, s32[304]{0:T(512)S(4)}, s32[304]{0:T(512)S(4)}, s32[8,32]{1,0:T(8,128)S(4)}) custom-call(s32[1]{0:T(128)} %bitcast.me, s32[1]{0:T(128)} %bitcast.1.col, f32[16,120,128]{2,1,0:T(8,128)S(1)} %bitcast.9, f32[16,16,128]{2,1,0:T(8,128)S(1)} %get-tuple-element.29.mine, s32[16]{0:T(128)} %lev.3, ...), custom_call_target="tpu_custom_call" | custom-call | tf_op jit(solution)/shard_map/first/pallas_call | solution.py:569
  40.2 2.1 %all-to-all-done.1.rates = f32[16,96,128]{2,1,0:T(8,128)S(1)} async-done(((f32[16,96,128]{2,1,0:T(8,128)}), f32[16,96,128]{2,1,0:T(8,128)S(1)}, u32[]{:S(2)}, u32[]{:S(2)}) %all-to-all-start.1) | async-done | bytes 786464 | tf_op jit(solution)/shard_map/all_to_all | solution.py:554
  42.2 0.0 copy-start
  42.2 13.4 %all-to-all-start = ((f32[256,1,256]{2,1,0:T(1,128)}), f32[256,1,256]{2,1,0:T(1,128)S(1)}, u32[]{:S(2)}, u32[]{:S(2)}) async-start(f32[256,1,256]{2,1,0:T(1,128)} %bitcast.15), calls=%async_computation | async-start | bytes 524288 | tf_op jit(solution)/shard_map/all_to_all | solution.py:554
  55.7 6.1 %ahead1.1 = (f32[6,8,128]{2,1,0:T(8,128)S(1)}, s32[8,32]{1,0:T(8,128)S(4)}) custom-call(s32[8,32]{1,0:T(8,128)S(4)} %get-tuple-element.32.known, f32[16,120,128]{2,1,0:T(8,128)S(1)} %bitcast.10, f32[16,96,128]{2,1,0:T(8,128)S(1)} %all-to-all-done.1.rates, s32[304]{0:T(512)S(4)} %get-tuple-element.34.order, f32[17,8,128]{2,1,0:T(8,128)S(1)} %get-tuple-element.31.state.state_in), custom_call_target="tpu_custom_call" | custom-call | tf_op jit(solution)/shard_map/ahead1/pallas_call | solution.py:594
  61.8 0.0 copy-done
  61.8 9.4 %all-to-all-done.got = f32[256,1,256]{2,1,0:T(1,128)S(1)} async-done(((f32[256,1,256]{2,1,0:T(1,128)}), f32[256,1,256]{2,1,0:T(1,128)S(1)}, u32[]{:S(2)}, u32[]{:S(2)}) %all-to-all-start) | async-done | bytes 262176 | tf_op jit(solution)/shard_map/all_to_all | solution.py:554
  71.2 0.0 copy-start.1
  71.2 4.4 %after1.1 = (f32[17,8,128]{2,1,0:T(8,128)S(1)}, f32[96,8,128]{2,1,0:T(8,128)}, f32[8,8,256]{2,1,0:T(8,128)S(1)}) custom-call(f32[256,1,256]{2,1,0:T(1,128)S(1)} %all-to-all-done.got, f32[17,8,128]{2,1,0:T(8,128)S(1)} %get-tuple-element.31.state.state_in, f32[6,8,128]{2,1,0:T(8,128)S(1)} %get-tuple-element.35.sums, s32[8,32]{1,0:T(8,128)S(4)} %get-tuple-element.36.plan.rest_1_), custom_call_target="tpu_custom_call" | custom-call | tf_op jit(solution)/shard_map/after1/pallas_call | solution.py:617
  75.6 8.5 %all-to-all-start.2 = ((f32[256,1,384]{2,1,0:T(1,128)}), f32[256,1,384]{2,1,0:T(1,128)S(1)}, u32[]{:S(2)}, u32[]{:S(2)}) async-start(f32[256,1,384]{2,1,0:T(1,128)} %bitcast.14), calls=%async_computation.2 | async-start | bytes 786432 | tf_op jit(solution)/shard_map/all_to_all | solution.py:554
  84.1 0.0 copy-done.1
  84.1 8.9 %ahead2.1 = (f32[4,8,128]{2,1,0:T(8,128)S(1)}, s32[8,32]{1,0:T(8,128)S(4)}, f32[3,8,128]{2,1,0:T(8,128)S(1)}, f32[2,8,128]{2,1,0:T(8,128)S(1)}) custom-call(s32[8,32]{1,0:T(8,128)S(4)} %get-tuple-element.32.known, f32[16,120,128]{2,1,0:T(8,128)S(1)} %bitcast.11, f32[16,96,128]{2,1,0:T(8,128)S(1)} %copy-done.1, s32[304]{0:T(512)S(4)} %get-tuple-element.39.order, ...), custom_call_target="tpu_custom_call" | custom-call | tf_op jit(solution)/shard_map/ahead2/pallas_call | solution.py:594
  93.0 0.0 copy-start.2
  93.0 9.4 %all-to-all-done.2.got = f32[256,1,384]{2,1,0:T(1,128)S(1)} async-done(((f32[256,1,384]{2,1,0:T(1,128)}), f32[256,1,384]{2,1,0:T(1,128)S(1)}, u32[]{:S(2)}, u32[]{:S(2)}) %all-to-all-start.2) | async-done | bytes 393248 | tf_op jit(solution)/shard_map/all_to_all | solution.py:554
  102.5 5.2 %after2.1 = (f32[17,8,128]{2,1,0:T(8,128)S(1)}, f32[96,8,128]{2,1,0:T(8,128)}) custom-call(f32[256,1,384]{2,1,0:T(1,128)S(1)} %all-to-all-done.2.got, f32[17,8,128]{2,1,0:T(8,128)S(1)} %get-tuple-element.38.state.state_in, f32[4,8,128]{2,1,0:T(8,128)S(1)} %get-tuple-element.40.sums, s32[8,32]{1,0:T(8,128)S(4)} %get-tuple-element.41.plan, ...), custom_call_target="tpu_custom_call" | custom-call | tf_op jit(solution)/shard_map/after2/pallas_call | solution.py:617
  107.7 6.0 %all-to-all-start.3 = ((f32[256,1,384]{2,1,0:T(1,128)}), f32[256,1,384]{2,1,0:T(1,128)S(1)}, u32[]{:S(2)}, u32[]{:S(2)}) async-start(f32[256,1,384]{2,1,0:T(1,128)} %bitcast.13), calls=%async_computation.3 | async-start | bytes 786432 | tf_op jit(solution)/shard_map/all_to_all | solution.py:554
  113.7 0.0 copy-done.2
  113.7 5.8 %ahead3.1 = (f32[8,8,128]{2,1,0:T(8,128)S(1)}, s32[8,32]{1,0:T(8,128)S(4)}) custom-call(s32[8,32]{1,0:T(8,128)S(4)} %get-tuple-element.32.known, f32[16,120,128]{2,1,0:T(8,128)S(1)} %bitcast.12, f32[16,96,128]{2,1,0:T(8,128)S(1)} %copy-done.2, s32[304]{0:T(512)S(4)} %get-tuple-element.39.order, f32[17,8,128]{2,1,0:T(8,128)S(1)} %get-tuple-element.45.state.state_in, ...), custom_call_target="tpu_custom_call" | custom-call | tf_op jit(solution)/shard_map/ahead3/pallas_call | solution.py:594
  119.5 12.6 %all-to-all-done.3.got = f32[256,1,384]{2,1,0:T(1,128)S(1)} async-done(((f32[256,1,384]{2,1,0:T(1,128)}), f32[256,1,384]{2,1,0:T(1,128)S(1)}, u32[]{:S(2)}, u32[]{:S(2)}) %all-to-all-start.3) | async-done | bytes 393248 | tf_op jit(solution)/shard_map/all_to_all | solution.py:554
  132.1 0.0 copy-start.5
  132.1 5.7 %after3.1 = f32[16,1,1152]{2,1,0:T(1,128)S(1)} custom-call(f32[256,1,384]{2,1,0:T(1,128)S(1)} %all-to-all-done.3.got, f32[17,8,128]{2,1,0:T(8,128)S(1)} %get-tuple-element.45.state.state_in, f32[8,8,128]{2,1,0:T(8,128)S(1)} %get-tuple-element.47.sums, s32[8,32]{1,0:T(8,128)S(4)} %get-tuple-element.48.plan, f32[8,8,256]{2,1,0:T(8,128)S(1)} %get-tuple-element.42.rest_0_, ...), custom_call_target="tpu_custom_call" | custom-call | tf_op jit(solution)/shard_map/after3/pallas_call | solution.py:617
  137.9 0.0 copy-start.3
  137.9 0.0 copy-start.4
  137.9 12.4 %all_to_all.25.got = f32[16,1,1152]{2,1,0:T(1,128)S(1)} all-to-all(f32[16,1,1152]{2,1,0:T(1,128)S(1)} %after3.1), channel_id=1, replica_groups=mesh['blk'=16,'grp'=16] {'grp'}, dimensions={0} | all-to-all | bytes 147456 | tf_op jit(solution)/shard_map/all_to_all | solution.py:554
  150.3 0.0 copy-done.5
  150.3 0.0 copy-done.3
  150.3 0.0 copy-done.4
  150.3 1.3 last.1
Async XLA Ops:
  26.5 15.8 %all-to-all-start.1 = ((f32[16,96,128]{2,1,0:T(8,128)}), f32[16,96,128]{2,1,0:T(8,128)S(1)}, u32[]{:S(2)}, u32[]{:S(2)}) async-start(f32[16,96,128]{2,1,0:T(8,128)} %get-tuple-element.33), calls=%async_computation.1 | async-start | bytes 1572864 | tf_op jit(solution)/shard_map/all_to_all | solution.py:554
  42.2 19.5 %copy-start = (f32[16,96,128]{2,1,0:T(8,128)}, f32[16,96,128]{2,1,0:T(8,128)S(1)}, u32[]{:S(2)}) copy-start(f32[16,96,128]{2,1,0:T(8,128)S(1)} %all-to-all-done.1.rates) | copy-start | bytes 2359300
  42.2 29.0 %all-to-all-start = ((f32[256,1,256]{2,1,0:T(1,128)}), f32[256,1,256]{2,1,0:T(1,128)S(1)}, u32[]{:S(2)}, u32[]{:S(2)}) async-start(f32[256,1,256]{2,1,0:T(1,128)} %bitcast.15), calls=%async_computation | async-start | bytes 524288 | tf_op jit(solution)/shard_map/all_to_all | solution.py:554
  71.2 12.9 %copy-start.1 = (f32[16,96,128]{2,1,0:T(8,128)S(1)}, f32[16,96,128]{2,1,0:T(8,128)}, u32[]{:S(2)}) copy-start(f32[16,96,128]{2,1,0:T(8,128)} %copy-done) | copy-start | bytes 2359300
  75.6 26.8 %all-to-all-start.2 = ((f32[256,1,384]{2,1,0:T(1,128)}), f32[256,1,384]{2,1,0:T(1,128)S(1)}, u32[]{:S(2)}, u32[]{:S(2)}) async-start(f32[256,1,384]{2,1,0:T(1,128)} %bitcast.14), calls=%async_computation.2 | async-start | bytes 786432 | tf_op jit(solution)/shard_map/all_to_all | solution.py:554
  93.0 20.7 %copy-start.2 = (f32[16,96,128]{2,1,0:T(8,128)S(1)}, f32[16,96,128]{2,1,0:T(8,128)}, u32[]{:S(2)}) copy-start(f32[16,96,128]{2,1,0:T(8,128)} %copy-done) | copy-start | bytes 2359300
  107.7 24.5 %all-to-all-start.3 = ((f32[256,1,384]{2,1,0:T(1,128)}), f32[256,1,384]{2,1,0:T(1,128)S(1)}, u32[]{:S(2)}, u32[]{:S(2)}) async-start(f32[256,1,384]{2,1,0:T(1,128)} %bitcast.13), calls=%async_computation.3 | async-start | bytes 786432 | tf_op jit(solution)/shard_map/all_to_all | solution.py:554
  132.1 18.1 %copy-start.5 = (f32[6,2048]{1,0:T(8,128)S(1)}, f32[6,2048]{1,0:T(8,128)}, u32[]{:S(2)}) copy-start(f32[6,2048]{1,0:T(8,128)} %irr.1) | copy-start | bytes 147460
  137.9 12.4 %copy-start.3 = (f32[6,2048]{1,0:T(8,128)S(1)}, f32[6,2048]{1,0:T(8,128)}, u32[]{:S(2)}) copy-start(f32[6,2048]{1,0:T(8,128)} %ps.3) | copy-start | bytes 147460
  137.9 12.4 %copy-start.4 = (f32[6,2048]{1,0:T(8,128)S(1)}, f32[6,2048]{1,0:T(8,128)}, u32[]{:S(2)}) copy-start(f32[6,2048]{1,0:T(8,128)} %fr.3) | copy-start | bytes 147460
